TPU v7x, 256 devices: a whole 4x4x8 slice. The times are simulated.
256 devices in a mesh: group: 8 (over x_lo, y), member: 32 (over x_hi, z, core).
Axes of the slice: x: 4 (x_hi: 2, x_lo: 2; x = x_hi * 2 + x_lo), y: 4, z: 8, core: 2. Of those that a mesh axis runs over, the one named last changes fastest.
Arguments:
- entity: bfloat16 [65536, 800], P(('group', 'member')), may hold values from -3 to 7.5
- adagrad_state: float32 [65536], P(('group', 'member')), may hold values from 0.01 to 1
- relation: bfloat16 [1345, 800], replicated, may hold values from -1.8 to 1.8
- source_ids: int32 [2, 131072], P(None, ('group', 'member')), may hold values from 0 to 255
- relation_ids: int32 [2, 131072], P(None, ('group', 'member')), may hold values from 0 to 1344
- dest_groups: int32 [2, 131072, 1], P(None, ('group', 'member')), may hold values from 0 to 7; in each aligned block of 512 rows (0 to 511, 512 to 1023, ..., all dimensions but the last counted through in order) at most 128 rows name the same one
- dest_rows: int32 [2, 131072], P(None, ('group', 'member')), may hold values from 0 to 255
- negative_ids: int32 [2, 256000], P(None, ('group', 'member')), may hold values from 0 to 255
- owners: int32 [2, 8], replicated, may hold values from 0 to 31
Outputs:
- new_entity: bfloat16 [65536, 800], P(('group', 'member'))
- new_state: float32 [65536], P(('group', 'member'))
Inputs may be any that keep to these rules, and one draw needn't show every extreme that they name: `dest_groups`: for each sub-step and each device's 512 edges, at most 128 name any one destination group, a bound that some block reaches.
All inputs are finite; a program needn't handle non-finite values.
Results may differ from a plain program's by a relative error of at most 0.017.
Values may be sent and summed in bfloat16 or wider, within the bound.
A program may use at most 64 MiB of HBM per device.

v0:
```python
import jax
import jax.numpy as jnp
from jax import lax
from jax.sharding import PartitionSpec as P


def broadcast(value, axis, source):
    kept = jnp.where(lax.axis_index(axis) == source, value, 0).astype(value.dtype)
    return lax.psum(kept, axis)


def complex_query(source, rel):
    half = source.shape[-1] // 2
    sr, si = (source[..., :half], source[..., half:])
    rr, ri = (rel[..., :half], rel[..., half:])
    return jnp.concatenate([sr * rr - si * ri, sr * ri + si * rr], -1)


def source_grad(grad_query, rel):
    half = grad_query.shape[-1] // 2
    gr, gi = (grad_query[..., :half], grad_query[..., half:])
    rr, ri = (rel[..., :half], rel[..., half:])
    return jnp.concatenate([gr * rr + gi * ri, gi * rr - gr * ri], -1)


def edge_terms(source_rows, rel_rows, dest_rows, negatives):
    rel = rel_rows.astype(jnp.float32)
    query = complex_query(source_rows.astype(jnp.float32), rel).astype(jnp.bfloat16)
    dest = dest_rows.astype(jnp.float32)
    positive = jnp.sum(query.astype(jnp.float32) * dest, -1)
    scores = lax.dot_general(
        query, negatives, (((1,), (1,)), ((), ())), preferred_element_type=jnp.float32
    )
    top = jnp.maximum(jnp.max(scores, 1), positive)
    pos_exp = jnp.exp(positive - top)
    neg_exp = jnp.exp(scores - top[:, None])
    total = pos_exp + jnp.sum(neg_exp, 1)
    coef_pos = pos_exp / total - 1.0
    coef_neg = (neg_exp / total[:, None]).astype(jnp.bfloat16)
    grad_query = coef_pos[:, None] * dest + jnp.dot(
        coef_neg, negatives, preferred_element_type=jnp.float32
    )
    grad_source = source_grad(grad_query, rel)
    grad_neg = lax.dot_general(
        coef_neg, query, (((0,), (0,)), ((), ())), preferred_element_type=jnp.float32
    )
    return (grad_source, query, coef_pos, grad_neg)


def scatter_rows(values, row_ids, count):
    onehot = (row_ids[:, None] == jnp.arange(count, dtype=jnp.int32)[None, :]).astype(jnp.float32)
    return lax.dot_general(
        onehot,
        values,
        (((0,), (0,)), ((), ())),
        precision=lax.Precision.HIGHEST,
        preferred_element_type=jnp.float32,
    )


def per_device(
    entity,
    adagrad_state,
    relation,
    source_ids,
    relation_ids,
    dest_groups,
    dest_rows,
    negative_ids,
    owners,
):
    groups = lax.axis_size("group")
    group_index = lax.axis_index("group")
    member_index = lax.axis_index("member")
    shard_rows = entity.shape[0]
    table = entity
    state = adagrad_state
    for step in range(source_ids.shape[0]):
        root = owners[step, group_index]
        block = broadcast(table, "member", root)
        src = source_ids[step]
        rel = relation_ids[step]
        dgr = dest_groups[step, :, 0]
        drw = dest_rows[step]
        neg = negative_ids[step]
        source_rows = jnp.take(block, src, axis=0)
        rel_rows = jnp.take(relation, rel, axis=0)
        negatives = jnp.take(table, neg, axis=0)
        whole = lax.all_gather(table, "group", axis=0, tiled=True)
        flat = dgr * shard_rows + drw
        dest_vals = jnp.take(whole, flat, axis=0)
        grad_source, query, coef_pos, grad_neg = edge_terms(
            source_rows, rel_rows, dest_vals, negatives
        )
        grad_dest = coef_pos[:, None] * query.astype(jnp.float32)
        spread = scatter_rows(grad_dest, flat, groups * shard_rows)
        dest_total = lax.psum_scatter(spread, "group", scatter_dimension=0, tiled=True)
        source_part = scatter_rows(grad_source, src, shard_rows)
        source_total = lax.psum(source_part, "member")
        neg_total = scatter_rows(grad_neg, neg, shard_rows)
        grads = dest_total + neg_total + jnp.where(member_index == root, source_total, 0.0)
        state = state + jnp.mean(grads * grads, -1)
        table = (table.astype(jnp.float32) - 1.0 * grads / jnp.sqrt(state)[:, None]).astype(
            jnp.bfloat16
        )
    return (table, state)


def solution(mesh):
    placed = (
        P(("group", "member"), None),
        P(("group", "member")),
        P(),
        P(None, ("group", "member")),
        P(None, ("group", "member")),
        P(None, ("group", "member"), None),
        P(None, ("group", "member")),
        P(None, ("group", "member")),
        P(),
    )
    return jax.shard_map(
        per_device,
        mesh=mesh,
        in_specs=placed,
        out_specs=(P(("group", "member"), None), P(("group", "member"))),
        check_vma=False,
    )
```

profile of v0, /device:TPU:13, one launch (start us, length us, event | category | flops | bytes accessed | tf_op | source)
XLA Modules:
  0.0 1119.5 jit_solution(834115604931892025)
XLA Ops:
  11.0 2.0 copy.15
  14.0 5.3 gather_fusion.3
  19.3 3.4 copy.13
  22.8 2.1 gather_fusion.1
  26.3 244.0 %all-reduce.5.cloned.1.call-done = bf16[256,800]{0,1:T(8,128)(2,1)} async-done(((bf16[256,800]{0,1:T(8,128)(2,1)}), bf16[256,800]{0,1:T(8,128)(2,1)}) %all-reduce.5.cloned.1.call-update) | async-done | bytes 409616 | tf_op jit(solution)/shard_map/psum | solution.py:9
  271.5 2.8 gather_fusion
  274.2 2.3 copy.12
  279.9 2.6 fusion.44
  282.5 5.0 gather_fusion.2
  288.8 1.8 fusion.6
  290.7 1.9 fusion.4
  292.6 3.0 fusion.7
  296.0 1.9 fusion.10
  298.2 7.7 fusion
  306.6 4.7 fusion.38
  311.3 243.9 %all-reduce.7.cloned.1.call-done = f32[256,800]{0,1:T(8,128)} async-done(((f32[256,800]{0,1:T(8,128)}), f32[256,800]{0,1:T(8,128)}) %all-reduce.7.cloned.1.call-update) | async-done | bytes 819216 | tf_op jit(solution)/shard_map/psum | solution.py:99
  555.2 5.4 multiply_reduce_fusion.1
  562.7 2.1 gather_fusion.5
  567.7 5.3 gather_fusion.7
  573.0 243.6 %all-reduce.9.cloned.1.call-done = bf16[256,800]{0,1:T(8,128)(2,1)} async-done(((bf16[256,800]{0,1:T(8,128)(2,1)}), bf16[256,800]{0,1:T(8,128)(2,1)}) %all-reduce.9.cloned.1.call-update) | async-done | bytes 409616 | tf_op jit(solution)/shard_map/psum | solution.py:9
  817.8 2.1 gather_fusion.4
  824.0 2.6 fusion.45
  826.7 6.0 copy.22
  832.6 5.0 gather_fusion.6
  839.0 1.7 fusion.8
  840.7 1.9 fusion.5
  842.6 2.9 fusion.9
  845.9 1.9 fusion.14
  848.2 7.7 fusion.1
  857.5 3.1 fusion.37
  860.6 244.7 %all-reduce.11.cloned.1.call-done = f32[256,800]{0,1:T(8,128)} async-done(((f32[256,800]{0,1:T(8,128)}), f32[256,800]{0,1:T(8,128)}) %all-reduce.11.cloned.1.call-update) | async-done | bytes 819216 | tf_op jit(solution)/shard_map/psum | solution.py:99
  1105.3 5.4 multiply_reduce_fusion
  (124 shorter events, 26.5 us)
Async XLA Ops:
  8.0 5.1 copy-start.19
  8.0 262.2 %all-reduce.5.cloned.1.call-start = ((), (), s32[]{:S(2)}) async-start(), calls=%async_computation.2 | async-start | bytes 819200 | tf_op jit(solution)/shard_map/psum | solution.py:9
  10.9 271.6 %all-gather.3.cloned.1.call-start = ((), (), s32[]{:S(2)}) async-start(), calls=%async_computation.3 | async-start | bytes 4128768 | tf_op jit(solution)/shard_map/all_gather | solution.py:89
  13.0 1.0 copy-start
  13.0 542.2 %all-reduce.7.cloned.1.call-start = ((), (), s32[]{:S(2)}) async-start(), calls=%async_computation.5 | async-start | bytes 1638400 | tf_op jit(solution)/shard_map/psum | solution.py:99
  19.3 3.4 copy-start.21
  22.8 3.4 copy-start.22
  22.8 3.4 copy-start.23
  22.8 3.4 copy-start.24
  274.2 2.3 copy-start.7
  277.9 1.2 copy-start.1
  277.9 2.1 copy-start.11
  279.1 0.9 copy-start.15
  288.8 3.8 copy-start.5
  288.8 3.8 copy-start.8
  292.6 3.0 copy-start.2
  296.0 2.2 copy-start.14
  296.0 2.2 copy-start.16
  298.0 257.3 %reduce-scatter.3.cloned.1.call-start = ((), (), s32[]{:S(2)}) async-start(), calls=%async_computation.4 | async-start | bytes 7372800 | tf_op jit(solution)/shard_map/reduce_scatter | solution.py:97
  305.9 510.6 %all-reduce.9.cloned.1.call-start = ((), (), s32[]{:S(2)}) async-start(), calls=%async_computation.6 | async-start | bytes 819200 | tf_op jit(solution)/shard_map/psum | solution.py:9
  311.3 249.4 %copy-start.20 = (f32[256]{0:T(256)S(1)}, f32[256]{0:T(256)}, u32[]{:S(2)}) copy-start(f32[256]{0:T(256)} %param.18) | copy-start | bytes 3076
  311.3 249.4 %copy-start.4 = (bf16[256,800]{0,1:T(8,128)(2,1)S(1)}, bf16[256,800]{0,1:T(8,128)(2,1)}, u32[]{:S(2)}) copy-start(bf16[256,800]{0,1:T(8,128)(2,1)} %param.17) | copy-start | bytes 1228804
  561.8 264.8 %all-gather.5.cloned.1.call-start = ((), (), s32[]{:S(2)}) async-start(), calls=%async_computation.7 | async-start | bytes 3686400 | tf_op jit(solution)/shard_map/all_gather | solution.py:89
  562.4 542.9 %all-reduce.11.cloned.1.call-start = ((), (), s32[]{:S(2)}) async-start(), calls=%async_computation.9 | async-start | bytes 1638400 | tf_op jit(solution)/shard_map/psum | solution.py:99
  564.8 2.7 copy-start.3
  822.4 1.6 copy-start.12
  822.9 3.8 copy-start.17
  839.0 3.7 copy-start.6
  839.0 3.7 copy-start.9
  845.9 2.3 copy-start.18
  847.9 257.4 %reduce-scatter.5.cloned.1.call-start = ((), (), s32[]{:S(2)}) async-start(), calls=%async_computation.8 | async-start | bytes 7372800 | tf_op jit(solution)/shard_map/reduce_scatter | solution.py:97
  855.9 1.6 copy-start.10
  (1 other events, 0.8 us)
Sparse Core Ops, SparseCore 0:
  12.0 258.1 all-reduce.4
  298.1 257.1 all-reduce.6
  561.9 254.5 all-reduce.8
  848.0 257.2 all-reduce.10
Sparse Core Ops, SparseCore 1:
  13.3 51.7 all-gather.2
  306.0 74.9 reduce-scatter.2
  564.1 51.4 all-gather.4
  856.0 74.9 reduce-scatter.4
where the time goes:
time: 1120 us
  waiting for transfers between devices  977 us (87%)
  local copies, waits for them, and re-layouts  59 us (5%)
  matrix products  48.9 us (4%)
  between operations  17.3 us (2%)
  other arithmetic  16.4 us (1%)
    psum x2, waiting for transfers between devices, per_device(): source_total = lax.psum(source_part, 'member')  489 us
    psum x2, waiting for transfers between devices, broadcast(): return lax.psum(kept, axis)  488 us
    dot_general x6, matrix products, scatter_rows(): lax.dot_general(onehot, values, (((0,), (0,)), ((), ())), precision=lax.P...  30.1 us
  transfers between devices with their start and end apart: 8, of which 4 were waited for; matrix products, arithmetic and copies ran while one was open for 6% of the time, Pallas kernels for 0%

commit v1 on v0

v1 whole, which is shorter than its diff:
```python
import functools

import jax
import jax.numpy as jnp
from jax import lax
from jax.experimental import pallas as pl
from jax.experimental.pallas import tpu as pltpu
from jax.sharding import PartitionSpec as P

MESH = pl.DeviceIdType.MESH
F32 = jnp.float32
BF16 = jnp.bfloat16
LANES = 128
CAP = 128
LOW = -1e30


def dot_nn(a, b):
    return lax.dot_general(a, b, (((1,), (0,)), ((), ())), preferred_element_type=F32)


def dot_nt(a, b):
    return lax.dot_general(a, b, (((1,), (1,)), ((), ())), preferred_element_type=F32)


def dot_tn(a, b):
    return lax.dot_general(a, b, (((0,), (0,)), ((), ())), preferred_element_type=F32)


def iota(shape, dim):
    return lax.broadcasted_iota(jnp.int32, shape, dim)


def onehot(mask):
    return jnp.where(mask, 1.0, 0.0).astype(BF16)


def complex_parts(value, main):
    return value[:, :main], value[:, main : 2 * main], value[:, 2 * main :]


def tail_forms(tail, first):
    swapped = pltpu.roll(tail, LANES // 2, 1)
    return jnp.where(first, tail, swapped), jnp.where(first, swapped, tail)


def times(source, rel, main, first, sign):
    sr, si, st = complex_parts(source, main)
    rr, ri, rt = complex_parts(rel, main)
    tr, ti = tail_forms(rt, first)
    mixed = st * tr + sign * (pltpu.roll(st, LANES // 2, 1) * ti)
    return jnp.concatenate([sr * rr - si * ri, sr * ri + si * rr, mixed], 1)


def times_conjugate(grad, rel, main, first, sign):
    gr, gi, gt = complex_parts(grad, main)
    rr, ri, rt = complex_parts(rel, main)
    tr, ti = tail_forms(rt, first)
    mixed = gt * tr - sign * (pltpu.roll(gt, LANES // 2, 1) * ti)
    return jnp.concatenate([gr * rr + gi * ri, gi * rr - gr * ri, mixed], 1)


def kernel(
    groups,
    members,
    owners,
    entity,
    state_in,
    relation,
    source_ids,
    relation_ids,
    dest_groups,
    dest_rows,
    negative_ids,
    entity_out,
    state_out,
    place,
    table,
    state,
    rel_table,
    slot_src,
    slot_rel,
    src_rows,
    ids_send,
    ids_recv,
    counts,
    rel_slots,
    query,
    neg_exp,
    neg_max,
    neg_sum,
    weights,
    row_send,
    row_recv,
    grad_send,
    grad_recv,
    source_acc,
    grads,
    ar_in,
    ar_half,
    ar_mine,
    ar_parts,
    ar_piece,
    ar_other,
    ar_out,
    ids_ss,
    ids_rs,
    row_ss,
    row_rs,
    grad_ss,
    grad_rs,
    p1_ss,
    p1_rs,
    p2_ss,
    p2_rs,
    p3_ss,
    p3_rs,
    p4_ss,
    p4_rs,
    p5_ss,
    p5_rs,
):
    steps, edges = source_ids.shape
    rows, width = entity.shape
    rel_rows = relation.shape[0]
    half = width // 2
    main = half // LANES * LANES
    wide = table.shape[1]
    slots = groups * CAP
    depth = members // 4
    rings = groups // 2

    g = lax.axis_index("group")
    m = lax.axis_index("member")
    gx, gy = g // rings, g % rings
    core, z, xh = m % 2, (m // 2) % depth, m // (2 * depth)
    twin = m + 1 - 2 * core
    across = (m + 2 * depth) % members

    def peer(k):
        return ((gx + k // rings) % 2) * rings + (gy + k % rings) % rings

    def floor(k):
        return (z + k) % depth

    def along(other):
        return (g, xh * (2 * depth) + other * 2 + core)

    def remote(src, dst, send_sem, recv_sem, device):
        return pltpu.make_async_remote_copy(
            src_ref=src,
            dst_ref=dst,
            send_sem=send_sem,
            recv_sem=recv_sem,
            device_id=device,
            device_id_type=MESH,
        )

    barrier = pltpu.get_barrier_semaphore()

    @pl.loop(1, groups)
    def _(k):
        pl.semaphore_signal(barrier, inc=1, device_id=(peer(k), m), device_id_type=MESH)

    @pl.loop(1, depth)
    def _(k):
        pl.semaphore_signal(barrier, inc=1, device_id=along(floor(k)), device_id_type=MESH)

    pl.semaphore_signal(barrier, inc=1, device_id=(g, twin), device_id_type=MESH)
    pl.semaphore_signal(barrier, inc=1, device_id=(g, across), device_id_type=MESH)

    comp = iota((width, 1), 0)
    imag = comp >= half
    local = jnp.where(imag, comp - half, comp)
    spot = jnp.where(
        local < main,
        local + jnp.where(imag, main, 0),
        2 * main + jnp.where(imag, LANES // 2, 0) + local - main,
    )
    place[...] = onehot(iota((width, wide), 1) == spot)
    table[...] = dot_nn(entity[...], place[...]).astype(BF16)
    eye = iota((rows, rows), 0) == iota((rows, rows), 1)
    state[...] = jnp.sum(jnp.where(eye, state_in[...], 0.0), 1, keepdims=True)

    ids_send[...] = jnp.zeros_like(ids_send)
    for s in range(steps):
        group_row = dest_groups[s : s + 1, :]
        named = iota((16, edges), 0) == group_row
        before = onehot(iota((edges, edges), 0) < iota((edges, edges), 1))
        rank = dot_nn(onehot(named), before)
        rank = jnp.sum(jnp.where(named, rank, 0.0), 0, keepdims=True)
        slot_row = group_row * CAP + rank.astype(jnp.int32)
        taken = onehot(iota((slots, edges), 0) == slot_row)
        rel_row = relation_ids[s : s + 1, :]
        high = rel_row // 32
        which = iota((16, edges), 0)
        facts = jnp.where(which == 0, source_ids[s : s + 1, :], 0)
        facts = jnp.where(which == 1, high, facts)
        facts = jnp.where(which == 2, rel_row - 32 * high, facts)
        facts = jnp.where(which == 3, dest_rows[s : s + 1, :], facts)
        facts = jnp.where(which == 4, 1, facts)
        facts = facts.astype(F32).astype(BF16)
        flat = dot_nt(facts, taken).astype(jnp.int32)
        tall = dot_nt(taken, facts).astype(jnp.int32)
        empty_flat = flat[4:5, :] - 1
        empty_tall = tall[:, 4:5] - 1
        src_rows[s] = flat[0:1, :] + 4 * rows * empty_flat
        slot_src[s] = tall[:, 0:1] + 4 * rows * empty_tall
        slot_rel[s] = 32 * tall[:, 1:2] + tall[:, 2:3] + 4 * rel_rows * empty_tall
        wanted = flat[3:4, :] + 4 * rows * empty_flat
        for d in range(groups):
            ids_send[d, s : s + 1, :] = wanted[:, d * CAP : (d + 1) * CAP]

    pl.semaphore_wait(barrier, groups + depth)

    def ids_copy(d):
        return remote(ids_send.at[d], ids_recv.at[g], ids_ss.at[d], ids_rs.at[g], (d, m))

    def ids_arrival(d):
        return remote(ids_send.at[d], ids_recv.at[d], ids_ss.at[d], ids_rs.at[d], (d, m))

    @pl.loop(1, groups)
    def _(k):
        ids_copy(peer(k)).start()

    ids_recv[g] = ids_send[g]
    rel_table[...] = dot_nn(relation[...], place[...]).astype(BF16)

    @pl.loop(1, groups)
    def _(k):
        d = peer(k)
        ids_copy(d).wait_send()
        ids_arrival(d).wait_recv()

    first = iota((1, LANES), 1) < LANES // 2
    sign = jnp.where(first, -1.0, 1.0)

    def ar_start(i):
        remote(
            ar_in.at[i, 1 - core], ar_half.at[i], p1_ss.at[i], p1_rs.at[i], (g, twin)
        ).start()

    def ar_scatter_copy(i, other):
        return remote(
            ar_mine.at[i, other],
            ar_parts.at[i, z],
            p2_ss.at[i, other],
            p2_rs.at[i, z],
            along(other),
        )

    def ar_scatter_arrival(i, other):
        return remote(
            ar_mine.at[i, other],
            ar_parts.at[i, other],
            p2_ss.at[i, other],
            p2_rs.at[i, other],
            along(other),
        )

    def ar_gather_copy(i, other):
        return remote(
            ar_out.at[i, core, z],
            ar_out.at[i, core, z],
            p4_ss.at[i, other],
            p4_rs.at[i, z],
            along(other),
        )

    def ar_gather_arrival(i, other):
        return remote(
            ar_out.at[i, core, other],
            ar_out.at[i, core, other],
            p4_ss.at[i, other],
            p4_rs.at[i, other],
            along(other),
        )

    def ar_scatter(i):
        remote(
            ar_in.at[i, 1 - core], ar_half.at[i], p1_ss.at[i], p1_rs.at[i], (g, twin)
        ).wait()
        mine = ar_in[i, core].astype(F32) + ar_half[i].astype(F32)
        ar_mine[i] = mine.astype(BF16).reshape(depth, rows // 2 // depth, wide)

        @pl.loop(1, depth)
        def _(k):
            ar_scatter_copy(i, floor(k)).start()

    def ar_cross(i):
        @pl.loop(1, depth)
        def _(k):
            other = floor(k)
            ar_scatter_copy(i, other).wait_send()
            ar_scatter_arrival(i, other).wait_recv()

        ar_parts[i, z] = ar_mine[i, z]
        piece = jnp.sum(ar_parts[i].astype(F32), 0)
        ar_piece[i] = piece.astype(BF16)
        copy = remote(ar_piece.at[i], ar_other.at[i], p3_ss.at[i], p3_rs.at[i], (g, across))
        copy.start()
        copy.wait()
        whole = ar_piece[i].astype(F32) + ar_other[i].astype(F32)
        ar_out[i, core, z] = whole.astype(BF16)

        @pl.loop(1, depth)
        def _(k):
            ar_gather_copy(i, floor(k)).start()

    def ar_finish(i):
        @pl.loop(1, depth)
        def _(k):
            other = floor(k)
            ar_gather_copy(i, other).wait_send()
            ar_gather_arrival(i, other).wait_recv()

        out = remote(
            ar_out.at[i, core], ar_out.at[i, core], p5_ss.at[i], p5_rs.at[i], (g, twin)
        )
        back = remote(
            ar_out.at[i, 1 - core], ar_out.at[i, 1 - core], p5_ss.at[i], p5_rs.at[i], (g, twin)
        )
        out.start()
        out.wait_send()
        back.wait_recv()

    @pl.loop(0, steps)
    def _(s):
        root = owners[s, g]
        fetch, reduce = 2 * s, 2 * s + 1
        kept = jnp.where(m == root, table[...].astype(F32), 0.0).astype(BF16)
        ar_in[fetch] = kept.reshape(2, rows // 2, wide)
        ar_start(fetch)

        def row_copy(d):
            return remote(
                row_send.at[s, d], row_recv.at[s, g], row_ss.at[s, d], row_rs.at[s, g], (d, m)
            )

        def row_arrival(d):
            return remote(
                row_send.at[s, d], row_recv.at[s, d], row_ss.at[s, d], row_rs.at[s, d], (d, m)
            )

        def grad_copy(d):
            return remote(
                grad_send.at[s, d], grad_recv.at[s, g], grad_ss.at[s, d], grad_rs.at[s, g], (d, m)
            )

        def grad_arrival(d):
            return remote(
                grad_send.at[s, d], grad_recv.at[s, d], grad_ss.at[s, d], grad_rs.at[s, d], (d, m)
            )

        def asked(d):
            return onehot(iota((rows, CAP), 0) == ids_recv[d, pl.ds(s, 1), :])

        @pl.loop(1, groups)
        def _(k):
            d = peer(k)
            row_send[s, d] = dot_tn(asked(d), table[...]).astype(BF16)
            row_copy(d).start()

        row_recv[s, g] = dot_tn(asked(g), table[...]).astype(BF16)
        ar_scatter(fetch)

        slot_count = negative_ids.shape[1]
        hits = onehot(iota((rows, slot_count), 0) == negative_ids[pl.ds(s, 1), :])
        counts[...] = dot_nt(jnp.ones((8, slot_count), BF16), hits)

        def relations(k):
            base = pl.multiple_of(k * 2 * CAP, 2 * CAP)
            chosen = onehot(iota((2 * CAP, rel_rows), 1) == slot_rel[s, pl.ds(base, 2 * CAP), :])
            rel_slots[pl.ds(base, 2 * CAP), :] = dot_nn(chosen, rel_table[...]).astype(BF16)

        @pl.loop(0, groups // 4)
        def _(k):
            relations(k)

        ar_cross(fetch)

        @pl.loop(groups // 4, groups // 2)
        def _(k):
            relations(k)

        ar_finish(fetch)

        count_row = counts[0:1, :]
        present = count_row > 0.5

        @pl.loop(0, groups)
        def _(d):
            base = pl.multiple_of(d * CAP, CAP)
            here = pl.ds(base, CAP)
            chosen = onehot(iota((CAP, rows), 1) == slot_src[s, here, :])
            source = dot_nn(chosen, ar_out[fetch].reshape(rows, wide))
            q = times(source, rel_slots[here, :].astype(F32), main, first, sign).astype(BF16)
            query[here, :] = q
            scores = jnp.where(present, dot_nt(q, table[...]), LOW)
            top = jnp.max(scores, 1, keepdims=True)
            e = jnp.exp(scores - top) * count_row
            neg_exp[here, :] = e
            neg_max[here, :] = top
            neg_sum[here, :] = jnp.sum(e, 1, keepdims=True)

        source_acc[...] = jnp.zeros_like(source_acc)

        @pl.loop(0, groups)
        def _(k):
            d = peer(k)

            @pl.when(k > 0)
            def _():
                row_copy(d).wait_send()
                row_arrival(d).wait_recv()

            base = pl.multiple_of(d * CAP, CAP)
            here = pl.ds(base, CAP)
            q = query[here, :].astype(F32)
            dest = row_recv[s, d].astype(F32)
            positive = jnp.sum(q * dest, 1, keepdims=True)
            low = neg_max[here, :]
            top = jnp.maximum(low, positive)
            pos_exp = jnp.exp(positive - top)
            shrink = jnp.exp(low - top)
            total = pos_exp + neg_sum[here, :] * shrink
            coef_pos = pos_exp / total - 1.0
            grad_send[s, d] = (coef_pos * q).astype(BF16)

            @pl.when(k > 0)
            def _():
                grad_copy(d).start()

            coef_neg = (neg_exp[here, :] * (shrink / total)).astype(BF16)
            weights[here, :] = coef_neg
            grad_query = coef_pos * dest + dot_nn(coef_neg, table[...])
            grad_source = times_conjugate(
                grad_query, rel_slots[here, :].astype(F32), main, first, sign
            ).astype(BF16)
            spread = onehot(iota((rows, CAP), 0) == src_rows[s, :, here])
            source_acc[...] += dot_nn(spread, grad_source)

        ar_in[reduce] = source_acc[...].astype(BF16).reshape(2, rows // 2, wide)
        ar_start(reduce)
        grad_recv[s, g] = grad_send[s, g]
        ar_scatter(reduce)
        grads[...] = dot_tn(weights[...], query[...])
        ar_cross(reduce)
        ar_finish(reduce)

        @pl.loop(1, groups)
        def _(k):
            d = peer(k)
            grad_copy(d).wait_send()
            grad_arrival(d).wait_recv()

        @pl.loop(0, groups)
        def _(d):
            grads[...] += dot_nn(asked(d), grad_recv[s, d])

        total = grads[...] + jnp.where(
            m == root, ar_out[reduce].reshape(rows, wide).astype(F32), 0.0
        )
        fresh = state[...] + jnp.sum(total * total, 1, keepdims=True) * (1.0 / width)
        state[...] = fresh
        table[...] = (table[...].astype(F32) - total / jnp.sqrt(fresh)).astype(BF16)

    entity_out[...] = dot_nt(table[...], place[...]).astype(BF16)
    state_out[...] = jnp.sum(jnp.where(eye, state[...], 0.0), 0, keepdims=True)


def per_device(
    groups,
    members,
    entity,
    adagrad_state,
    relation,
    source_ids,
    relation_ids,
    dest_groups,
    dest_rows,
    negative_ids,
    owners,
):
    rows, width = entity.shape
    steps, edges = source_ids.shape
    half = width // 2
    wide = 2 * (half // LANES * LANES) + LANES
    slots = groups * CAP
    depth = members // 4
    piece = rows // 2 // depth
    uses = 2 * steps
    dma = pltpu.SemaphoreType.DMA
    vmem = pltpu.VMEM
    whole = pl.BlockSpec(memory_space=pltpu.VMEM)
    table, state = pl.pallas_call(
        functools.partial(kernel, groups, members),
        out_shape=(
            jax.ShapeDtypeStruct((rows, width), BF16),
            jax.ShapeDtypeStruct((1, rows), F32),
        ),
        in_specs=[pl.BlockSpec(memory_space=pltpu.SMEM)] + [whole] * 8,
        out_specs=(whole, whole),
        scratch_shapes=[
            vmem((width, wide), BF16),
            vmem((rows, wide), BF16),
            vmem((rows, 1), F32),
            vmem((relation.shape[0], wide), BF16),
            vmem((steps, slots, 1), jnp.int32),
            vmem((steps, slots, 1), jnp.int32),
            vmem((steps, 1, slots), jnp.int32),
            vmem((groups, 8, CAP), jnp.int32),
            vmem((groups, 8, CAP), jnp.int32),
            vmem((8, rows), F32),
            vmem((slots, wide), BF16),
            vmem((slots, wide), BF16),
            vmem((slots, rows), F32),
            vmem((slots, 1), F32),
            vmem((slots, 1), F32),
            vmem((slots, rows), BF16),
            vmem((steps, groups, CAP, wide), BF16),
            vmem((steps, groups, CAP, wide), BF16),
            vmem((steps, groups, CAP, wide), BF16),
            vmem((steps, groups, CAP, wide), BF16),
            vmem((rows, wide), F32),
            vmem((rows, wide), F32),
            vmem((uses, 2, rows // 2, wide), BF16),
            vmem((uses, rows // 2, wide), BF16),
            vmem((uses, depth, piece, wide), BF16),
            vmem((uses, depth, piece, wide), BF16),
            vmem((uses, piece, wide), BF16),
            vmem((uses, piece, wide), BF16),
            vmem((uses, 2, depth, piece, wide), BF16),
            dma((groups,)),
            dma((groups,)),
            dma((steps, groups)),
            dma((steps, groups)),
            dma((steps, groups)),
            dma((steps, groups)),
            dma((uses,)),
            dma((uses,)),
            dma((uses, depth)),
            dma((uses, depth)),
            dma((uses,)),
            dma((uses,)),
            dma((uses, depth)),
            dma((uses, depth)),
            dma((uses,)),
            dma((uses,)),
        ],
        compiler_params=pltpu.CompilerParams(
            collective_id=0, has_side_effects=True, vmem_limit_bytes=60 << 20
        ),
    )(
        owners,
        entity,
        adagrad_state.reshape(1, rows),
        relation,
        source_ids,
        relation_ids,
        dest_groups.reshape(steps, edges),
        dest_rows,
        negative_ids,
    )
    return (table, state.reshape(rows))


def solution(mesh):
    placed = (
        P(("group", "member"), None),
        P(("group", "member")),
        P(),
        P(None, ("group", "member")),
        P(None, ("group", "member")),
        P(None, ("group", "member"), None),
        P(None, ("group", "member")),
        P(None, ("group", "member")),
        P(),
    )
    return jax.shard_map(
        functools.partial(per_device, mesh.shape["group"], mesh.shape["member"]),
        mesh=mesh,
        in_specs=placed,
        out_specs=(P(("group", "member"), None), P(("group", "member"))),
        check_vma=False,
    )
```

time: 1120 us -> 185 us (0.17)
  waiting for transfers between devices: 977 us -> 0 us
  Pallas kernels: 0 us -> 172 us
  matrix products: 48.9 us -> 0 us
  local copies, waits for them, and re-layouts: 59 us -> 10.7 us
  between operations: 17.3 us -> 0.64 us
  other arithmetic: 16.4 us -> 0 us
    psum x4 -> x0, waiting for transfers between devices: 976 us -> none  [the longest x2 489 us: per_device(): source_total = lax.psum(source_part, 'member')]
    pallas_call x0 -> x1, Pallas kernels: none -> 172 us  [per_device(): pl.pallas_call(functools.partial(kernel, groups, members), out_shape=(jax...]
    dot_general x12 -> x0, matrix products: 48.9 us -> none  [the longest x6 30.1 us: scatter_rows(): lax.dot_general(onehot, values, (((0,), (0,)), ((), ())), precision=lax.P...]
    gather x14 -> x0, local copies, waits for them, and re-layouts: 38.1 us -> none  [the longest x4 12.6 us: per_device(): dest_vals = jnp.take(whole, flat, axis=0)]
  transfers between devices with their start and end apart: 8 -> 0, of which waited for: 4 -> 0; matrix products, arithmetic and copies ran while one was open for 6% -> 0% of each run, Pallas kernels for 0% -> 0%
where the time goes in v1:
time: 185 us; the launch traced here: 183 us
  Pallas kernels  172 us (93%)
  local copies, waits for them, and re-layouts  10.7 us (6%)
    pallas_call x1, Pallas kernels, per_device(): pl.pallas_call(functools.partial(kernel, groups, members), out_shape=(jax...  172 us
    unnamed x5, local copies, waits for them, and re-layouts  10.7 us

profile of v1, /device:TPU:13, one launch (start us, length us, event | category | flops | bytes accessed | tf_op | source)
XLA Modules:
  0.0 183.3 jit_solution(6579848142821333493)
XLA Ops:
  0.6 1.3 copy.16
  1.9 2.0 %copy.11.entity = bf16[256,800]{1,0:T(8,128)(2,1)} copy(bf16[256,800]{0,1:T(8,128)(2,1)} %param.9) | data formatting | bytes 819200 | tf_op args[0]
  3.9 4.3 %copy.12.relation = bf16[1345,800]{1,0:T(8,128)(2,1)} copy(bf16[1345,800]{0,1:T(8,128)(2,1)} %param.11) | data formatting | bytes 4304000 | tf_op args[2]
  8.2 171.9 %shard_map.104 = (bf16[256,800]{1,0:T(8,128)(2,1)}, f32[1,256]{1,0:T(1,128)}) custom-call(s32[2,8]{1,0:T(2,128)} %owners.1, bf16[256,800]{1,0:T(8,128)(2,1)} %copy.11.entity, f32[1,256]{1,0:T(1,128)} %bitcast.6, bf16[1345,800]{1,0:T(8,128)(2,1)} %copy.12.relation, s32[2,512]{1,0:T(2,128)} %source_ids.1, s32[2,512]{1,0:T(2,128)} %relation_ids.1, ...), custom_call_target="tpu_custom_call" | custom-call | tf_op jit(solution)/shard_map/pallas_call | solution.py:496
  180.1 2.0 %copy.13 = bf16[256,800]{0,1:T(8,128)(2,1)} copy(bf16[256,800]{1,0:T(8,128)(2,1)} %get-tuple-element.6) | data formatting | bytes 819200
  182.1 1.2 copy.18

commit v2 on v1

--- a/solution.py
+++ b/solution.py
@@ -81,6 +81,7 @@
     slot_src,
     slot_rel,
     src_rows,
+    taken,
     ids_send,
     ids_recv,
     counts,
@@ -121,8 +122,8 @@
     p5_rs,
 ):
     steps, edges = source_ids.shape
-    rows, width = entity.shape
-    rel_rows = relation.shape[0]
+    width, rows = entity.shape
+    rel_rows = relation.shape[1]
     half = width // 2
     main = half // LANES * LANES
     wide = table.shape[1]
@@ -139,6 +140,9 @@
 
     def peer(k):
         return ((gx + k // rings) % 2) * rings + (gy + k % rings) % rings
+
+    def mirror(k):
+        return k // rings * rings + (rings - k % rings) % rings
 
     def floor(k):
         return (z + k) % depth
@@ -158,14 +162,10 @@
 
     barrier = pltpu.get_barrier_semaphore()
 
-    @pl.loop(1, groups)
-    def _(k):
+    for k in range(1, groups):
         pl.semaphore_signal(barrier, inc=1, device_id=(peer(k), m), device_id_type=MESH)
-
-    @pl.loop(1, depth)
-    def _(k):
+    for k in range(1, depth):
         pl.semaphore_signal(barrier, inc=1, device_id=along(floor(k)), device_id_type=MESH)
-
     pl.semaphore_signal(barrier, inc=1, device_id=(g, twin), device_id_type=MESH)
     pl.semaphore_signal(barrier, inc=1, device_id=(g, across), device_id_type=MESH)
 
@@ -178,19 +178,23 @@
         2 * main + jnp.where(imag, LANES // 2, 0) + local - main,
     )
     place[...] = onehot(iota((width, wide), 1) == spot)
-    table[...] = dot_nn(entity[...], place[...]).astype(BF16)
+    table[...] = dot_tn(entity[...], place[...]).astype(BF16)
     eye = iota((rows, rows), 0) == iota((rows, rows), 1)
     state[...] = jnp.sum(jnp.where(eye, state_in[...], 0.0), 1, keepdims=True)
-
-    ids_send[...] = jnp.zeros_like(ids_send)
-    for s in range(steps):
-        group_row = dest_groups[s : s + 1, :]
-        named = iota((16, edges), 0) == group_row
-        before = onehot(iota((edges, edges), 0) < iota((edges, edges), 1))
-        rank = dot_nn(onehot(named), before)
-        rank = jnp.sum(jnp.where(named, rank, 0.0), 0, keepdims=True)
-        slot_row = group_row * CAP + rank.astype(jnp.int32)
-        taken = onehot(iota((slots, edges), 0) == slot_row)
+    first = iota((1, LANES), 1) < LANES // 2
+    sign = jnp.where(first, -1.0, 1.0)
+
+    pl.semaphore_wait(barrier, groups + depth)
+
+    def ids_copy(k):
+        return remote(
+            ids_send.at[k], ids_recv.at[mirror(k)], ids_ss.at[k], ids_rs.at[mirror(k)], (peer(k), m)
+        )
+
+    def ids_arrival(k):
+        return remote(ids_send.at[k], ids_recv.at[k], ids_ss.at[k], ids_rs.at[k], (peer(k), m))
+
+    def edge_facts(s):
         rel_row = relation_ids[s : s + 1, :]
         high = rel_row // 32
         which = iota((16, edges), 0)
@@ -199,46 +203,47 @@
         facts = jnp.where(which == 2, rel_row - 32 * high, facts)
         facts = jnp.where(which == 3, dest_rows[s : s + 1, :], facts)
         facts = jnp.where(which == 4, 1, facts)
-        facts = facts.astype(F32).astype(BF16)
-        flat = dot_nt(facts, taken).astype(jnp.int32)
-        tall = dot_nt(taken, facts).astype(jnp.int32)
-        empty_flat = flat[4:5, :] - 1
-        empty_tall = tall[:, 4:5] - 1
-        src_rows[s] = flat[0:1, :] + 4 * rows * empty_flat
-        slot_src[s] = tall[:, 0:1] + 4 * rows * empty_tall
-        slot_rel[s] = 32 * tall[:, 1:2] + tall[:, 2:3] + 4 * rel_rows * empty_tall
-        wanted = flat[3:4, :] + 4 * rows * empty_flat
-        for d in range(groups):
-            ids_send[d, s : s + 1, :] = wanted[:, d * CAP : (d + 1) * CAP]
-
-    pl.semaphore_wait(barrier, groups + depth)
-
-    def ids_copy(d):
-        return remote(ids_send.at[d], ids_recv.at[g], ids_ss.at[d], ids_rs.at[g], (d, m))
-
-    def ids_arrival(d):
-        return remote(ids_send.at[d], ids_recv.at[d], ids_ss.at[d], ids_rs.at[d], (d, m))
-
-    @pl.loop(1, groups)
-    def _(k):
-        ids_copy(peer(k)).start()
-
-    ids_recv[g] = ids_send[g]
-    rel_table[...] = dot_nn(relation[...], place[...]).astype(BF16)
-
-    @pl.loop(1, groups)
-    def _(k):
-        d = peer(k)
-        ids_copy(d).wait_send()
-        ids_arrival(d).wait_recv()
-
-    first = iota((1, LANES), 1) < LANES // 2
-    sign = jnp.where(first, -1.0, 1.0)
-
-    def ar_start(i):
-        remote(
+        return facts.astype(F32).astype(BF16)
+
+    def assign_slots():
+        ids_send[...] = jnp.zeros_like(ids_send)
+        before = onehot(iota((edges, edges), 0) < iota((edges, edges), 1))
+        for s in range(steps):
+            group_row = dest_groups[s]
+            hop_x = (group_row // rings + 2 - gx) % 2
+            hop_y = (group_row % rings + rings - gy) % rings
+            hop = hop_x * rings + hop_y
+            named = iota((16, edges), 0) == hop
+            rank = dot_nn(onehot(named), before)
+            rank = jnp.sum(jnp.where(named, rank, 0.0), 0, keepdims=True)
+            slot_row = hop * CAP + rank.astype(jnp.int32)
+            taken[s] = onehot(iota((slots, edges), 0) == slot_row)
+            flat = dot_nt(edge_facts(s), taken[s]).astype(jnp.int32)
+            empty = flat[4:5, :] - 1
+            src_rows[s] = flat[0:1, :] + 4 * rows * empty
+            wanted = flat[3:4, :] + 4 * rows * empty
+            for k in range(groups):
+                ids_send[k, s : s + 1, :] = wanted[:, k * CAP : (k + 1) * CAP]
+        for k in range(1, groups):
+            ids_copy(k).start()
+        ids_recv[0] = ids_send[0]
+
+    def slot_columns():
+        for s in range(steps):
+            tall = dot_nt(taken[s], edge_facts(s)).astype(jnp.int32)
+            empty = tall[:, 4:5] - 1
+            slot_src[s] = tall[:, 0:1] + 4 * rows * empty
+            slot_rel[s] = 32 * tall[:, 1:2] + tall[:, 2:3] + 4 * rel_rows * empty
+
+    def ids_wait():
+        for k in range(1, groups):
+            ids_copy(k).wait_send()
+            ids_arrival(k).wait_recv()
+
+    def ar_first(i):
+        return remote(
             ar_in.at[i, 1 - core], ar_half.at[i], p1_ss.at[i], p1_rs.at[i], (g, twin)
-        ).start()
+        )
 
     def ar_scatter_copy(i, other):
         return remote(
@@ -258,6 +263,9 @@
             along(other),
         )
 
+    def ar_cross_copy(i):
+        return remote(ar_piece.at[i], ar_other.at[i], p3_ss.at[i], p3_rs.at[i], (g, across))
+
     def ar_gather_copy(i, other):
         return remote(
             ar_out.at[i, core, z],
@@ -276,10 +284,13 @@
             along(other),
         )
 
+    def ar_last(i, which):
+        return remote(
+            ar_out.at[i, which], ar_out.at[i, which], p5_ss.at[i], p5_rs.at[i], (g, twin)
+        )
+
     def ar_scatter(i):
-        remote(
-            ar_in.at[i, 1 - core], ar_half.at[i], p1_ss.at[i], p1_rs.at[i], (g, twin)
-        ).wait()
+        ar_first(i).wait()
         mine = ar_in[i, core].astype(F32) + ar_half[i].astype(F32)
         ar_mine[i] = mine.astype(BF16).reshape(depth, rows // 2 // depth, wide)
 
@@ -297,9 +308,10 @@
         ar_parts[i, z] = ar_mine[i, z]
         piece = jnp.sum(ar_parts[i].astype(F32), 0)
         ar_piece[i] = piece.astype(BF16)
-        copy = remote(ar_piece.at[i], ar_other.at[i], p3_ss.at[i], p3_rs.at[i], (g, across))
-        copy.start()
-        copy.wait()
+        ar_cross_copy(i).start()
+
+    def ar_gather(i):
+        ar_cross_copy(i).wait()
         whole = ar_piece[i].astype(F32) + ar_other[i].astype(F32)
         ar_out[i, core, z] = whole.astype(BF16)
 
@@ -307,92 +319,135 @@
         def _(k):
             ar_gather_copy(i, floor(k)).start()
 
-    def ar_finish(i):
+    def ar_share(i):
         @pl.loop(1, depth)
         def _(k):
             other = floor(k)
             ar_gather_copy(i, other).wait_send()
             ar_gather_arrival(i, other).wait_recv()
 
-        out = remote(
-            ar_out.at[i, core], ar_out.at[i, core], p5_ss.at[i], p5_rs.at[i], (g, twin)
-        )
-        back = remote(
-            ar_out.at[i, 1 - core], ar_out.at[i, 1 - core], p5_ss.at[i], p5_rs.at[i], (g, twin)
-        )
-        out.start()
-        out.wait_send()
-        back.wait_recv()
+        ar_last(i, core).start()
+
+    def ar_done(i):
+        ar_last(i, core).wait_send()
+        ar_last(i, 1 - core).wait_recv()
 
     @pl.loop(0, steps)
     def _(s):
         root = owners[s, g]
         fetch, reduce = 2 * s, 2 * s + 1
-        kept = jnp.where(m == root, table[...].astype(F32), 0.0).astype(BF16)
-        ar_in[fetch] = kept.reshape(2, rows // 2, wide)
-        ar_start(fetch)
-
-        def row_copy(d):
+
+        def row_copy(k):
             return remote(
-                row_send.at[s, d], row_recv.at[s, g], row_ss.at[s, d], row_rs.at[s, g], (d, m)
+                row_send.at[s, k],
+                row_recv.at[s, mirror(k)],
+                row_ss.at[s, k],
+                row_rs.at[s, mirror(k)],
+                (peer(k), m),
             )
 
-        def row_arrival(d):
+        def row_arrival(k):
             return remote(
-                row_send.at[s, d], row_recv.at[s, d], row_ss.at[s, d], row_rs.at[s, d], (d, m)
+                row_send.at[s, k], row_recv.at[s, k], row_ss.at[s, k], row_rs.at[s, k], (peer(k), m)
             )
 
-        def grad_copy(d):
+        def grad_copy(k):
             return remote(
-                grad_send.at[s, d], grad_recv.at[s, g], grad_ss.at[s, d], grad_rs.at[s, g], (d, m)
+                grad_send.at[s, k],
+                grad_recv.at[s, mirror(k)],
+                grad_ss.at[s, k],
+                grad_rs.at[s, mirror(k)],
+                (peer(k), m),
             )
 
-        def grad_arrival(d):
+        def grad_arrival(k):
             return remote(
-                grad_send.at[s, d], grad_recv.at[s, d], grad_ss.at[s, d], grad_rs.at[s, d], (d, m)
+                grad_send.at[s, k],
+                grad_recv.at[s, k],
+                grad_ss.at[s, k],
+                grad_rs.at[s, k],
+                (peer(k), m),
             )
 
-        def asked(d):
-            return onehot(iota((rows, CAP), 0) == ids_recv[d, pl.ds(s, 1), :])
-
-        @pl.loop(1, groups)
-        def _(k):
-            d = peer(k)
-            row_send[s, d] = dot_tn(asked(d), table[...]).astype(BF16)
-            row_copy(d).start()
-
-        row_recv[s, g] = dot_tn(asked(g), table[...]).astype(BF16)
-        ar_scatter(fetch)
-
-        slot_count = negative_ids.shape[1]
-        hits = onehot(iota((rows, slot_count), 0) == negative_ids[pl.ds(s, 1), :])
-        counts[...] = dot_nt(jnp.ones((8, slot_count), BF16), hits)
+        def asked(p):
+            ids = [ids_recv[2 * p + j, pl.ds(s, 1), :] for j in range(2)]
+            return onehot(iota((rows, 2 * CAP), 0) == jnp.concatenate(ids, 1))
+
+        def pick_rows(p):
+            picked = dot_tn(asked(p), table[...]).astype(BF16)
+            row_send[s, 2 * p : 2 * p + 2] = picked.reshape(2, CAP, wide)
+
+        def send_rows(p):
+            for k in (2 * p, 2 * p + 1):
+                if k:
+                    row_copy(k).start()
 
         def relations(k):
             base = pl.multiple_of(k * 2 * CAP, 2 * CAP)
             chosen = onehot(iota((2 * CAP, rel_rows), 1) == slot_rel[s, pl.ds(base, 2 * CAP), :])
             rel_slots[pl.ds(base, 2 * CAP), :] = dot_nn(chosen, rel_table[...]).astype(BF16)
 
+        ar_in[fetch] = (
+            jnp.where(m == root, table[...].astype(F32), 0.0).astype(BF16)
+        ).reshape(2, rows // 2, wide)
+        ar_first(fetch).start()
+
+        @pl.when(s == 0)
+        def _():
+            assign_slots()
+
+        @pl.when(s > 0)
+        def _():
+            pick_rows(2)
+            send_rows(2)
+
+        ar_scatter(fetch)
+
+        @pl.when(s == 0)
+        def _():
+            slot_columns()
+            ids_wait()
+            pick_rows(2)
+            send_rows(2)
+
+        pick_rows(0)
+        send_rows(0)
+        row_recv[s, 0] = row_send[s, 0]
+        pick_rows(1)
+        send_rows(1)
+        pick_rows(3)
+
+        @pl.when(s == 0)
+        def _():
+            rel_table[...] = dot_tn(relation[...], place[...]).astype(BF16)
+
+        slot_count = negative_ids.shape[1]
+        hits = onehot(iota((rows, slot_count), 0) == negative_ids[pl.ds(s, 1), :])
+        counts[...] = dot_nt(jnp.ones((8, slot_count), BF16), hits)
+        ar_cross(fetch)
+        send_rows(3)
+
         @pl.loop(0, groups // 4)
         def _(k):
             relations(k)
 
-        ar_cross(fetch)
+        ar_gather(fetch)
 
         @pl.loop(groups // 4, groups // 2)
         def _(k):
             relations(k)
 
-        ar_finish(fetch)
-
+        ar_share(fetch)
+        source_acc[...] = jnp.zeros_like(source_acc)
         count_row = counts[0:1, :]
         present = count_row > 0.5
-
-        @pl.loop(0, groups)
-        def _(d):
-            base = pl.multiple_of(d * CAP, CAP)
-            here = pl.ds(base, CAP)
-            chosen = onehot(iota((CAP, rows), 1) == slot_src[s, here, :])
+        ar_done(fetch)
+
+        @pl.loop(0, groups // 2)
+        def _(p):
+            base = pl.multiple_of(p * 2 * CAP, 2 * CAP)
+            here = pl.ds(base, 2 * CAP)
+            chosen = onehot(iota((2 * CAP, rows), 1) == slot_src[s, here, :])
             source = dot_nn(chosen, ar_out[fetch].reshape(rows, wide))
             q = times(source, rel_slots[here, :].astype(F32), main, first, sign).astype(BF16)
             query[here, :] = q
@@ -403,21 +458,22 @@
             neg_max[here, :] = top
             neg_sum[here, :] = jnp.sum(e, 1, keepdims=True)
 
-        source_acc[...] = jnp.zeros_like(source_acc)
-
-        @pl.loop(0, groups)
-        def _(k):
-            d = peer(k)
-
-            @pl.when(k > 0)
-            def _():
-                row_copy(d).wait_send()
-                row_arrival(d).wait_recv()
-
-            base = pl.multiple_of(d * CAP, CAP)
-            here = pl.ds(base, CAP)
+        @pl.loop(0, groups // 2)
+        def _(turn):
+            p = (turn + 2) % 3 * (1 - turn // 3) + turn // 3 * 3
+
+            for j in range(2):
+
+                @pl.when(2 * p + j > 0)
+                def _():
+                    row_copy(2 * p + j).wait_send()
+                    row_arrival(2 * p + j).wait_recv()
+
+            base = pl.multiple_of(p * 2 * CAP, 2 * CAP)
+            here = pl.ds(base, 2 * CAP)
+            pair = pl.ds(2 * p, 2)
             q = query[here, :].astype(F32)
-            dest = row_recv[s, d].astype(F32)
+            dest = row_recv[s, pair].reshape(2 * CAP, wide).astype(F32)
             positive = jnp.sum(q * dest, 1, keepdims=True)
             low = neg_max[here, :]
             top = jnp.maximum(low, positive)
@@ -425,11 +481,13 @@
             shrink = jnp.exp(low - top)
             total = pos_exp + neg_sum[here, :] * shrink
             coef_pos = pos_exp / total - 1.0
-            grad_send[s, d] = (coef_pos * q).astype(BF16)
-
-            @pl.when(k > 0)
-            def _():
-                grad_copy(d).start()
+            grad_send[s, pair] = (coef_pos * q).astype(BF16).reshape(2, CAP, wide)
+
+            for j in range(2):
+
+                @pl.when((2 * p + j > 0) & (p < 3))
+                def _():
+                    grad_copy(2 * p + j).start()
 
             coef_neg = (neg_exp[here, :] * (shrink / total)).astype(BF16)
             weights[here, :] = coef_neg
@@ -437,27 +495,33 @@
             grad_source = times_conjugate(
                 grad_query, rel_slots[here, :].astype(F32), main, first, sign
             ).astype(BF16)
-            spread = onehot(iota((rows, CAP), 0) == src_rows[s, :, here])
+            spread = onehot(iota((rows, 2 * CAP), 0) == src_rows[s, :, here])
             source_acc[...] += dot_nn(spread, grad_source)
 
         ar_in[reduce] = source_acc[...].astype(BF16).reshape(2, rows // 2, wide)
-        ar_start(reduce)
-        grad_recv[s, g] = grad_send[s, g]
+        ar_first(reduce).start()
+        grad_recv[s, 0] = grad_send[s, 0]
         ar_scatter(reduce)
         grads[...] = dot_tn(weights[...], query[...])
         ar_cross(reduce)
-        ar_finish(reduce)
-
-        @pl.loop(1, groups)
-        def _(k):
-            d = peer(k)
-            grad_copy(d).wait_send()
-            grad_arrival(d).wait_recv()
-
-        @pl.loop(0, groups)
-        def _(d):
-            grads[...] += dot_nn(asked(d), grad_recv[s, d])
-
+        grad_copy(6).start()
+        grad_copy(7).start()
+        ar_gather(reduce)
+
+        def scatter_grads(p):
+            for k in (2 * p, 2 * p + 1):
+                if k:
+                    grad_copy(k).wait_send()
+                    grad_arrival(k).wait_recv()
+            arrived = grad_recv[s, 2 * p : 2 * p + 2].reshape(2 * CAP, wide)
+            grads[...] += dot_nn(asked(p), arrived)
+
+        scatter_grads(2)
+        scatter_grads(0)
+        scatter_grads(1)
+        ar_share(reduce)
+        scatter_grads(3)
+        ar_done(reduce)
         total = grads[...] + jnp.where(
             m == root, ar_out[reduce].reshape(rows, wide).astype(F32), 0.0
         )
@@ -465,7 +529,7 @@
         state[...] = fresh
         table[...] = (table[...].astype(F32) - total / jnp.sqrt(fresh)).astype(BF16)
 
-    entity_out[...] = dot_nt(table[...], place[...]).astype(BF16)
+    entity_out[...] = dot_nt(place[...], table[...]).astype(BF16)
     state_out[...] = jnp.sum(jnp.where(eye, state[...], 0.0), 0, keepdims=True)
 
 
@@ -496,7 +560,7 @@
     table, state = pl.pallas_call(
         functools.partial(kernel, groups, members),
         out_shape=(
-            jax.ShapeDtypeStruct((rows, width), BF16),
+            jax.ShapeDtypeStruct((width, rows), BF16),
             jax.ShapeDtypeStruct((1, rows), F32),
         ),
         in_specs=[pl.BlockSpec(memory_space=pltpu.SMEM)] + [whole] * 8,
@@ -509,6 +573,7 @@
             vmem((steps, slots, 1), jnp.int32),
             vmem((steps, slots, 1), jnp.int32),
             vmem((steps, 1, slots), jnp.int32),
+            vmem((steps, slots, edges), BF16),
             vmem((groups, 8, CAP), jnp.int32),
             vmem((groups, 8, CAP), jnp.int32),
             vmem((8, rows), F32),
@@ -553,16 +618,16 @@
         ),
     )(
         owners,
-        entity,
+        entity.T,
         adagrad_state.reshape(1, rows),
-        relation,
+        relation.T,
         source_ids,
         relation_ids,
-        dest_groups.reshape(steps, edges),
+        jnp.transpose(dest_groups, (0, 2, 1)),
         dest_rows,
         negative_ids,
     )
-    return (table, state.reshape(rows))
+    return (table.T, state.reshape(rows))
 
 
 def solution(mesh):

time: 185 us -> 136 us (0.74)
  Pallas kernels: 172 us -> 132 us
  local copies, waits for them, and re-layouts: 10.7 us -> 3.02 us
    pallas_call x1, Pallas kernels: 172 us -> 132 us  [per_device(): pl.pallas_call(functools.partial(kernel, groups, members), out_shape=(jax...]
    unnamed x5 -> x2, local copies, waits for them, and re-layouts: 10.7 us -> 3.02 us
where the time goes in v2:
time: 136 us; the launch traced here: 135 us
  Pallas kernels  132 us (97%)
  local copies, waits for them, and re-layouts  3.02 us (2%)
    pallas_call x1, Pallas kernels, per_device(): pl.pallas_call(functools.partial(kernel, groups, members), out_shape=(jax...  132 us
    unnamed x2, local copies, waits for them, and re-layouts  3.02 us

profile of v2, /device:TPU:13, one launch (start us, length us, event | category | flops | bytes accessed | tf_op | source)
XLA Modules:
  0.0 135.2 jit_solution(5384967216796667438)
XLA Ops:
  0.6 131.6 %shard_map.104 = (bf16[800,256]{1,0:T(8,128)(2,1)}, f32[1,256]{1,0:T(1,128)}) custom-call(s32[2,8]{1,0:T(2,128)} %owners.1, bf16[800,256]{1,0:T(8,128)(2,1)} %bitcast.7, f32[1,256]{1,0:T(1,128)} %bitcast.10, bf16[800,1345]{1,0:T(8,128)(2,1)} %bitcast.6, s32[2,512]{1,0:T(2,128)} %source_ids.1, s32[2,512]{1,0:T(2,128)} %relation_ids.1, s32[2,1,512]{2,1,0:T(1,128)} %bitcast.9, ...), custom_call_target="tpu_custom_call" | custom-call | tf_op jit(solution)/shard_map/pallas_call | solution.py:560
  132.2 1.8 %copy.13 = bf16[256,800]{0,1:T(8,128)(2,1)} copy(bf16[256,800]{0,1:T(8,128)(2,1)} %bitcast.8) | data formatting | bytes 819200
  134.0 1.2 copy.14

commit v3 on v2

--- a/solution.py
+++ b/solution.py
@@ -58,6 +58,29 @@
     tr, ti = tail_forms(rt, first)
     mixed = gt * tr - sign * (pltpu.roll(gt, LANES // 2, 1) * ti)
     return jnp.concatenate([gr * rr + gi * ri, gi * rr - gr * ri, mixed], 1)
+
+
+def pack(value, main, tail):
+    count = value.shape[0]
+    part = count // (LANES // 2 // tail)
+    tiles = [value[:, c : c + LANES] for c in range(0, 2 * main, LANES)]
+    last = value[:, 2 * main :]
+    mixed = last[:part]
+    for j in range(1, count // part):
+        mixed = mixed + pltpu.roll(last[j * part : (j + 1) * part], tail * j, 1)
+    return jnp.concatenate(tiles + [mixed], 0)
+
+
+def unpack(stack, count, main, tail):
+    part = count // (LANES // 2 // tail)
+    tiles = 2 * main // LANES
+    mixed = stack[tiles * count : tiles * count + part]
+    used = iota((1, LANES), 1) % (LANES // 2) < tail
+    last = [jnp.where(used, mixed, 0.0)]
+    for j in range(1, count // part):
+        last.append(jnp.where(used, pltpu.roll(mixed, LANES - tail * j, 1), 0.0))
+    columns = [stack[c * count : (c + 1) * count] for c in range(tiles)]
+    return jnp.concatenate(columns + [jnp.concatenate(last, 0)], 1)
 
 
 def kernel(
@@ -95,6 +118,7 @@
     row_recv,
     grad_send,
     grad_recv,
+    block,
     source_acc,
     grads,
     ar_in,
@@ -127,6 +151,9 @@
     half = width // 2
     main = half // LANES * LANES
     wide = table.shape[1]
+    tail = half - main
+    share = rows // 2
+    piece = ar_half.shape[2]
     slots = groups * CAP
     depth = members // 4
     rings = groups // 2
@@ -183,8 +210,6 @@
     state[...] = jnp.sum(jnp.where(eye, state_in[...], 0.0), 1, keepdims=True)
     first = iota((1, LANES), 1) < LANES // 2
     sign = jnp.where(first, -1.0, 1.0)
-
-    pl.semaphore_wait(barrier, groups + depth)
 
     def ids_copy(k):
         return remote(
@@ -224,9 +249,12 @@
             wanted = flat[3:4, :] + 4 * rows * empty
             for k in range(groups):
                 ids_send[k, s : s + 1, :] = wanted[:, k * CAP : (k + 1) * CAP]
-        for k in range(1, groups):
-            ids_copy(k).start()
-        ids_recv[0] = ids_send[0]
+
+    assign_slots()
+    pl.semaphore_wait(barrier, groups + depth)
+    for k in range(1, groups):
+        ids_copy(k).start()
+    ids_recv[0] = ids_send[0]
 
     def slot_columns():
         for s in range(steps):
@@ -240,10 +268,35 @@
             ids_copy(k).wait_send()
             ids_arrival(k).wait_recv()
 
+    near = sorted(range(1, depth), key=lambda k: min(k, depth - k))
+    far = near[::-1]
+
+    def ar_fill(i, value):
+        for h in range(2):
+            stack = pack(value[h * share : (h + 1) * share], main, tail)
+            spare = jnp.zeros((depth * piece - stack.shape[0], LANES), F32)
+            stack = jnp.concatenate([stack, spare], 0)
+            ar_in[i, h] = stack.reshape(depth, piece, LANES).astype(BF16)
+
+    def ar_read(i):
+        halves = []
+        for h in range(2):
+            stack = ar_out[i, h].astype(F32).reshape(depth * piece, LANES)
+            halves.append(unpack(stack, share, main, tail))
+        return jnp.concatenate(halves, 0)
+
+    def ar_first_copy(i, other):
+        return remote(
+            ar_in.at[i, 1 - core, other],
+            ar_half.at[i, other],
+            p1_ss.at[i, other],
+            p1_rs.at[i, other],
+            (g, twin),
+        )
+
     def ar_first(i):
-        return remote(
-            ar_in.at[i, 1 - core], ar_half.at[i], p1_ss.at[i], p1_rs.at[i], (g, twin)
-        )
+        for k in far + [0]:
+            ar_first_copy(i, floor(k)).start()
 
     def ar_scatter_copy(i, other):
         return remote(
@@ -284,19 +337,23 @@
             along(other),
         )
 
-    def ar_last(i, which):
+    def ar_last(i, which, other):
         return remote(
-            ar_out.at[i, which], ar_out.at[i, which], p5_ss.at[i], p5_rs.at[i], (g, twin)
+            ar_out.at[i, which, other],
+            ar_out.at[i, which, other],
+            p5_ss.at[i, other],
+            p5_rs.at[i, other],
+            (g, twin),
         )
 
     def ar_scatter(i):
-        ar_first(i).wait()
-        mine = ar_in[i, core].astype(F32) + ar_half[i].astype(F32)
-        ar_mine[i] = mine.astype(BF16).reshape(depth, rows // 2 // depth, wide)
-
-        @pl.loop(1, depth)
-        def _(k):
-            ar_scatter_copy(i, floor(k)).start()
+        for k in far + [0]:
+            other = floor(k)
+            ar_first_copy(i, other).wait()
+            mine = ar_in[i, core, other].astype(F32) + ar_half[i, other].astype(F32)
+            ar_mine[i, other] = mine.astype(BF16)
+            if k:
+                ar_scatter_copy(i, other).start()
 
     def ar_cross(i):
         @pl.loop(1, depth)
@@ -314,23 +371,23 @@
         ar_cross_copy(i).wait()
         whole = ar_piece[i].astype(F32) + ar_other[i].astype(F32)
         ar_out[i, core, z] = whole.astype(BF16)
-
-        @pl.loop(1, depth)
-        def _(k):
+        for k in far:
             ar_gather_copy(i, floor(k)).start()
+        ar_last(i, core, z).start()
 
     def ar_share(i):
-        @pl.loop(1, depth)
-        def _(k):
+        for k in near:
             other = floor(k)
-            ar_gather_copy(i, other).wait_send()
             ar_gather_arrival(i, other).wait_recv()
-
-        ar_last(i, core).start()
+            ar_last(i, core, other).start()
 
     def ar_done(i):
-        ar_last(i, core).wait_send()
-        ar_last(i, 1 - core).wait_recv()
+        for k in [0] + near:
+            other = floor(k)
+            if k:
+                ar_gather_copy(i, other).wait_send()
+            ar_last(i, core, other).wait_send()
+            ar_last(i, 1 - core, other).wait_recv()
 
     @pl.loop(0, steps)
     def _(s):
@@ -374,8 +431,9 @@
             return onehot(iota((rows, 2 * CAP), 0) == jnp.concatenate(ids, 1))
 
         def pick_rows(p):
-            picked = dot_tn(asked(p), table[...]).astype(BF16)
-            row_send[s, 2 * p : 2 * p + 2] = picked.reshape(2, CAP, wide)
+            picked = dot_tn(asked(p), table[...])
+            for j in range(2):
+                row_send[s, 2 * p + j] = pack(picked[j * CAP : (j + 1) * CAP], main, tail).astype(BF16)
 
         def send_rows(p):
             for k in (2 * p, 2 * p + 1):
@@ -387,14 +445,8 @@
             chosen = onehot(iota((2 * CAP, rel_rows), 1) == slot_rel[s, pl.ds(base, 2 * CAP), :])
             rel_slots[pl.ds(base, 2 * CAP), :] = dot_nn(chosen, rel_table[...]).astype(BF16)
 
-        ar_in[fetch] = (
-            jnp.where(m == root, table[...].astype(F32), 0.0).astype(BF16)
-        ).reshape(2, rows // 2, wide)
-        ar_first(fetch).start()
-
-        @pl.when(s == 0)
-        def _():
-            assign_slots()
+        ar_fill(fetch, jnp.where(m == root, table[...].astype(F32), 0.0))
+        ar_first(fetch)
 
         @pl.when(s > 0)
         def _():
@@ -442,13 +494,14 @@
         count_row = counts[0:1, :]
         present = count_row > 0.5
         ar_done(fetch)
+        block[...] = ar_read(fetch).astype(BF16)
 
         @pl.loop(0, groups // 2)
         def _(p):
             base = pl.multiple_of(p * 2 * CAP, 2 * CAP)
             here = pl.ds(base, 2 * CAP)
             chosen = onehot(iota((2 * CAP, rows), 1) == slot_src[s, here, :])
-            source = dot_nn(chosen, ar_out[fetch].reshape(rows, wide))
+            source = dot_nn(chosen, block[...])
             q = times(source, rel_slots[here, :].astype(F32), main, first, sign).astype(BF16)
             query[here, :] = q
             scores = jnp.where(present, dot_nt(q, table[...]), LOW)
@@ -471,9 +524,10 @@
 
             base = pl.multiple_of(p * 2 * CAP, 2 * CAP)
             here = pl.ds(base, 2 * CAP)
-            pair = pl.ds(2 * p, 2)
             q = query[here, :].astype(F32)
-            dest = row_recv[s, pair].reshape(2 * CAP, wide).astype(F32)
+            dest = jnp.concatenate(
+                [unpack(row_recv[s, 2 * p + j].astype(F32), CAP, main, tail) for j in range(2)], 0
+            )
             positive = jnp.sum(q * dest, 1, keepdims=True)
             low = neg_max[here, :]
             top = jnp.maximum(low, positive)
@@ -481,7 +535,10 @@
             shrink = jnp.exp(low - top)
             total = pos_exp + neg_sum[here, :] * shrink
             coef_pos = pos_exp / total - 1.0
-            grad_send[s, pair] = (coef_pos * q).astype(BF16).reshape(2, CAP, wide)
+            grad_dest = coef_pos * q
+            for j in range(2):
+                stack = pack(grad_dest[j * CAP : (j + 1) * CAP], main, tail)
+                grad_send[s, 2 * p + j] = stack.astype(BF16)
 
             for j in range(2):
 
@@ -498,8 +555,8 @@
             spread = onehot(iota((rows, 2 * CAP), 0) == src_rows[s, :, here])
             source_acc[...] += dot_nn(spread, grad_source)
 
-        ar_in[reduce] = source_acc[...].astype(BF16).reshape(2, rows // 2, wide)
-        ar_first(reduce).start()
+        ar_fill(reduce, source_acc[...])
+        ar_first(reduce)
         grad_recv[s, 0] = grad_send[s, 0]
         ar_scatter(reduce)
         grads[...] = dot_tn(weights[...], query[...])
@@ -513,8 +570,8 @@
                 if k:
                     grad_copy(k).wait_send()
                     grad_arrival(k).wait_recv()
-            arrived = grad_recv[s, 2 * p : 2 * p + 2].reshape(2 * CAP, wide)
-            grads[...] += dot_nn(asked(p), arrived)
+            arrived = [unpack(grad_recv[s, k].astype(F32), CAP, main, tail) for k in (2 * p, 2 * p + 1)]
+            grads[...] += dot_nn(asked(p), jnp.concatenate(arrived, 0).astype(BF16))
 
         scatter_grads(2)
         scatter_grads(0)
@@ -522,9 +579,7 @@
         ar_share(reduce)
         scatter_grads(3)
         ar_done(reduce)
-        total = grads[...] + jnp.where(
-            m == root, ar_out[reduce].reshape(rows, wide).astype(F32), 0.0
-        )
+        total = grads[...] + jnp.where(m == root, ar_read(reduce), 0.0)
         fresh = state[...] + jnp.sum(total * total, 1, keepdims=True) * (1.0 / width)
         state[...] = fresh
         table[...] = (table[...].astype(F32) - total / jnp.sqrt(fresh)).astype(BF16)
@@ -552,7 +607,8 @@
     wide = 2 * (half // LANES * LANES) + LANES
     slots = groups * CAP
     depth = members // 4
-    piece = rows // 2 // depth
+    stack = CAP * width // LANES
+    piece = -(-rows // 2 * width // LANES // depth // 8) * 8
     uses = 2 * steps
     dma = pltpu.SemaphoreType.DMA
     vmem = pltpu.VMEM
@@ -583,35 +639,36 @@
             vmem((slots, 1), F32),
             vmem((slots, 1), F32),
             vmem((slots, rows), BF16),
-            vmem((steps, groups, CAP, wide), BF16),
-            vmem((steps, groups, CAP, wide), BF16),
-            vmem((steps, groups, CAP, wide), BF16),
-            vmem((steps, groups, CAP, wide), BF16),
+            vmem((steps, groups, stack, LANES), BF16),
+            vmem((steps, groups, stack, LANES), BF16),
+            vmem((steps, groups, stack, LANES), BF16),
+            vmem((steps, groups, stack, LANES), BF16),
+            vmem((rows, wide), BF16),
             vmem((rows, wide), F32),
             vmem((rows, wide), F32),
-            vmem((uses, 2, rows // 2, wide), BF16),
-            vmem((uses, rows // 2, wide), BF16),
-            vmem((uses, depth, piece, wide), BF16),
-            vmem((uses, depth, piece, wide), BF16),
-            vmem((uses, piece, wide), BF16),
-            vmem((uses, piece, wide), BF16),
-            vmem((uses, 2, depth, piece, wide), BF16),
+            vmem((uses, 2, depth, piece, LANES), BF16),
+            vmem((uses, depth, piece, LANES), BF16),
+            vmem((uses, depth, piece, LANES), BF16),
+            vmem((uses, depth, piece, LANES), BF16),
+            vmem((uses, piece, LANES), BF16),
+            vmem((uses, piece, LANES), BF16),
+            vmem((uses, 2, depth, piece, LANES), BF16),
             dma((groups,)),
             dma((groups,)),
             dma((steps, groups)),
             dma((steps, groups)),
             dma((steps, groups)),
             dma((steps, groups)),
-            dma((uses,)),
-            dma((uses,)),
+            dma((uses, depth)),
+            dma((uses, depth)),
             dma((uses, depth)),
             dma((uses, depth)),
             dma((uses,)),
             dma((uses,)),
             dma((uses, depth)),
             dma((uses, depth)),
-            dma((uses,)),
-            dma((uses,)),
+            dma((uses, depth)),
+            dma((uses, depth)),
         ],
         compiler_params=pltpu.CompilerParams(
             collective_id=0, has_side_effects=True, vmem_limit_bytes=60 << 20

time: 136 us -> 123 us (0.904)
  Pallas kernels: 132 us -> 120 us
    pallas_call x1, Pallas kernels: 132 us -> 120 us  [per_device(): pl.pallas_call(functools.partial(kernel, groups, members), out_shape=(jax...]
where the time goes in v3:
time: 123 us
  Pallas kernels  120 us (98%)
  local copies, waits for them, and re-layouts  3.02 us (2%)
    pallas_call x1, Pallas kernels, per_device(): pl.pallas_call(functools.partial(kernel, groups, members), out_shape=(jax...  120 us
    unnamed x2, local copies, waits for them, and re-layouts  3.02 us

profile of v3, /device:TPU:13, one launch (start us, length us, event | category | flops | bytes accessed | tf_op | source)
XLA Modules:
  0.0 123.3 jit_solution(3313143135633741583)
XLA Ops:
  0.6 119.7 %shard_map.104 = (bf16[800,256]{1,0:T(8,128)(2,1)}, f32[1,256]{1,0:T(1,128)}) custom-call(s32[2,8]{1,0:T(2,128)} %owners.1, bf16[800,256]{1,0:T(8,128)(2,1)} %bitcast.7, f32[1,256]{1,0:T(1,128)} %bitcast.10, bf16[800,1345]{1,0:T(8,128)(2,1)} %bitcast.6, s32[2,512]{1,0:T(2,128)} %source_ids.1, s32[2,512]{1,0:T(2,128)} %relation_ids.1, s32[2,1,512]{2,1,0:T(1,128)} %bitcast.9, ...), custom_call_target="tpu_custom_call" | custom-call | tf_op jit(solution)/shard_map/pallas_call | solution.py:616
  120.3 1.8 %copy.13 = bf16[256,800]{0,1:T(8,128)(2,1)} copy(bf16[256,800]{0,1:T(8,128)(2,1)} %bitcast.8) | data formatting | bytes 819200
  122.1 1.2 %copy.14 = f32[256]{0:T(256)} copy(f32[256]{0:T(256)} %bitcast.11) | data formatting | bytes 2048

commit v4 on v3

--- a/solution.py
+++ b/solution.py
@@ -101,19 +101,23 @@
     table,
     state,
     rel_table,
-    slot_src,
-    slot_rel,
-    src_rows,
+    edge_src,
+    edge_rel,
+    facts,
     taken,
+    given,
     ids_send,
     ids_recv,
     counts,
-    rel_slots,
+    rel_edges,
     query,
     neg_exp,
     neg_max,
     neg_sum,
     weights,
+    coef,
+    dest,
+    grad_dest,
     row_send,
     row_recv,
     grad_send,
@@ -165,11 +169,14 @@
     twin = m + 1 - 2 * core
     across = (m + 2 * depth) % members
 
+    hops = [(0, j) for j in range(rings)]
+    hops += sorted(((1, j) for j in range(rings)), key=lambda hop: -min(hop[1], rings - hop[1]))
+
     def peer(k):
-        return ((gx + k // rings) % 2) * rings + (gy + k % rings) % rings
+        return ((gx + hops[k][0]) % 2) * rings + (gy + hops[k][1]) % rings
 
     def mirror(k):
-        return k // rings * rings + (rings - k % rings) % rings
+        return hops.index((hops[k][0], -hops[k][1] % rings))
 
     def floor(k):
         return (z + k) % depth
@@ -195,6 +202,60 @@
         pl.semaphore_signal(barrier, inc=1, device_id=along(floor(k)), device_id_type=MESH)
     pl.semaphore_signal(barrier, inc=1, device_id=(g, twin), device_id_type=MESH)
     pl.semaphore_signal(barrier, inc=1, device_id=(g, across), device_id_type=MESH)
+
+    def ids_copy(s, k):
+        return remote(
+            ids_send.at[s, k],
+            ids_recv.at[s, mirror(k)],
+            ids_ss.at[s, k],
+            ids_rs.at[s, mirror(k)],
+            (peer(k), m),
+        )
+
+    def ids_arrival(s, k):
+        return remote(
+            ids_send.at[s, k], ids_recv.at[s, k], ids_ss.at[s, k], ids_rs.at[s, k], (peer(k), m)
+        )
+
+    def assign_slots(turns):
+        before = onehot(iota((edges, edges), 0) < iota((edges, edges), 1))
+        for s in turns:
+            group_row = dest_groups[s]
+            hop_x = (group_row // rings + 2 - gx) % 2
+            hop_y = (group_row % rings + rings - gy) % rings
+            where = hop_x * rings + hop_y
+            hop = jnp.zeros_like(where)
+            for k in range(groups):
+                hop = jnp.where(where == hops[k][0] * rings + hops[k][1], k, hop)
+            named = iota((16, edges), 0) == hop
+            rank = dot_nn(onehot(named), before)
+            rank = jnp.sum(jnp.where(named, rank, 0.0), 0, keepdims=True).astype(jnp.int32)
+            taken[s] = onehot(iota((slots, edges), 0) == hop * CAP + rank)
+            rel_row = relation_ids[s : s + 1, :]
+            high = rel_row // 32
+            which = iota((16, edges), 0)
+            known = jnp.where(which == 0, source_ids[s : s + 1, :], 0)
+            known = jnp.where(which == 1, high, known)
+            known = jnp.where(which == 2, rel_row - 32 * high, known)
+            known = jnp.where(which == 3, dest_rows[s : s + 1, :], known)
+            known = jnp.where(which == 4, 1, known)
+            known = jnp.where(which == 5, hop, known)
+            known = jnp.where(which == 6, rank, known)
+            facts[s] = known.astype(F32).astype(BF16)
+            flat = dot_nt(facts[s], taken[s]).astype(jnp.int32)
+            wanted = flat[3:4, :] + 4 * rows * (flat[4:5, :] - 1)
+            for k in range(groups):
+                ids_send[s, k] = jnp.broadcast_to(wanted[:, k * CAP : (k + 1) * CAP], (8, CAP))
+
+    def ids_start(turns):
+        for s in turns:
+            for k in range(1, groups):
+                ids_copy(s, k).start()
+            ids_recv[s, 0] = ids_send[s, 0]
+
+    assign_slots(range(1))
+    pl.semaphore_wait(barrier, groups + depth)
+    ids_start(range(1))
 
     comp = iota((width, 1), 0)
     imag = comp >= half
@@ -211,62 +272,19 @@
     first = iota((1, LANES), 1) < LANES // 2
     sign = jnp.where(first, -1.0, 1.0)
 
-    def ids_copy(k):
-        return remote(
-            ids_send.at[k], ids_recv.at[mirror(k)], ids_ss.at[k], ids_rs.at[mirror(k)], (peer(k), m)
-        )
-
-    def ids_arrival(k):
-        return remote(ids_send.at[k], ids_recv.at[k], ids_ss.at[k], ids_rs.at[k], (peer(k), m))
-
-    def edge_facts(s):
-        rel_row = relation_ids[s : s + 1, :]
-        high = rel_row // 32
-        which = iota((16, edges), 0)
-        facts = jnp.where(which == 0, source_ids[s : s + 1, :], 0)
-        facts = jnp.where(which == 1, high, facts)
-        facts = jnp.where(which == 2, rel_row - 32 * high, facts)
-        facts = jnp.where(which == 3, dest_rows[s : s + 1, :], facts)
-        facts = jnp.where(which == 4, 1, facts)
-        return facts.astype(F32).astype(BF16)
-
-    def assign_slots():
-        ids_send[...] = jnp.zeros_like(ids_send)
-        before = onehot(iota((edges, edges), 0) < iota((edges, edges), 1))
+    def edge_columns():
+        same = onehot(iota((edges, edges), 0) == iota((edges, edges), 1))
         for s in range(steps):
-            group_row = dest_groups[s]
-            hop_x = (group_row // rings + 2 - gx) % 2
-            hop_y = (group_row % rings + rings - gy) % rings
-            hop = hop_x * rings + hop_y
-            named = iota((16, edges), 0) == hop
-            rank = dot_nn(onehot(named), before)
-            rank = jnp.sum(jnp.where(named, rank, 0.0), 0, keepdims=True)
-            slot_row = hop * CAP + rank.astype(jnp.int32)
-            taken[s] = onehot(iota((slots, edges), 0) == slot_row)
-            flat = dot_nt(edge_facts(s), taken[s]).astype(jnp.int32)
-            empty = flat[4:5, :] - 1
-            src_rows[s] = flat[0:1, :] + 4 * rows * empty
-            wanted = flat[3:4, :] + 4 * rows * empty
-            for k in range(groups):
-                ids_send[k, s : s + 1, :] = wanted[:, k * CAP : (k + 1) * CAP]
-
-    assign_slots()
-    pl.semaphore_wait(barrier, groups + depth)
-    for k in range(1, groups):
-        ids_copy(k).start()
-    ids_recv[0] = ids_send[0]
-
-    def slot_columns():
-        for s in range(steps):
-            tall = dot_nt(taken[s], edge_facts(s)).astype(jnp.int32)
-            empty = tall[:, 4:5] - 1
-            slot_src[s] = tall[:, 0:1] + 4 * rows * empty
-            slot_rel[s] = 32 * tall[:, 1:2] + tall[:, 2:3] + 4 * rel_rows * empty
-
-    def ids_wait():
-        for k in range(1, groups):
-            ids_copy(k).wait_send()
-            ids_arrival(k).wait_recv()
+            tall = dot_nt(same, facts[s]).astype(jnp.int32)
+            edge_src[s] = tall[:, 0:1]
+            edge_rel[s] = 32 * tall[:, 1:2] + tall[:, 2:3]
+            given[s] = onehot(iota((edges, slots), 1) == CAP * tall[:, 5:6] + tall[:, 6:7])
+
+    def ids_wait(turns):
+        for s in turns:
+            for k in range(1, groups):
+                ids_copy(s, k).wait_send()
+                ids_arrival(s, k).wait_recv()
 
     near = sorted(range(1, depth), key=lambda k: min(k, depth - k))
     far = near[::-1]
@@ -427,7 +445,7 @@
             )
 
         def asked(p):
-            ids = [ids_recv[2 * p + j, pl.ds(s, 1), :] for j in range(2)]
+            ids = [ids_recv[s, 2 * p + j, 0:1, :] for j in range(2)]
             return onehot(iota((rows, 2 * CAP), 0) == jnp.concatenate(ids, 1))
 
         def pick_rows(p):
@@ -441,26 +459,46 @@
                     row_copy(k).start()
 
         def relations(k):
-            base = pl.multiple_of(k * 2 * CAP, 2 * CAP)
-            chosen = onehot(iota((2 * CAP, rel_rows), 1) == slot_rel[s, pl.ds(base, 2 * CAP), :])
-            rel_slots[pl.ds(base, 2 * CAP), :] = dot_nn(chosen, rel_table[...]).astype(BF16)
-
-        ar_fill(fetch, jnp.where(m == root, table[...].astype(F32), 0.0))
-        ar_first(fetch)
+            here = pl.ds(pl.multiple_of(k * 2 * CAP, 2 * CAP), 2 * CAP)
+            chosen = onehot(iota((2 * CAP, rel_rows), 1) == edge_rel[s, here, :])
+            rel_edges[here, :] = dot_nn(chosen, rel_table[...]).astype(BF16)
+
+        def collect(p):
+            for k in (2 * p, 2 * p + 1):
+                if k:
+                    row_copy(k).wait_send()
+                    row_arrival(k).wait_recv()
+            arrived = [unpack(row_recv[s, k].astype(F32), CAP, main, tail) for k in (2 * p, 2 * p + 1)]
+            arrived = jnp.concatenate(arrived, 0).astype(BF16)
+            sorted_rows = dot_nn(given[s, :, 2 * p * CAP : (2 * p + 2) * CAP], arrived)
+            dest[...] = sorted_rows if p == 0 else dest[...] + sorted_rows
+
+        def make_grads(p):
+            block_rows = taken[s, 2 * p * CAP : (2 * p + 2) * CAP, :]
+            spread = dot_nn(block_rows, grad_dest[...])
+            for j in range(2):
+                stack = pack(spread[j * CAP : (j + 1) * CAP], main, tail)
+                grad_send[s, 2 * p + j] = stack.astype(BF16)
+
+        def send_grads(p):
+            for k in (2 * p, 2 * p + 1):
+                if k:
+                    grad_copy(k).start()
 
         @pl.when(s > 0)
         def _():
             pick_rows(2)
             send_rows(2)
 
+        ar_fill(fetch, jnp.where(m == root, table[...].astype(F32), 0.0))
+        ar_first(fetch)
         ar_scatter(fetch)
 
         @pl.when(s == 0)
         def _():
-            slot_columns()
-            ids_wait()
+            ids_wait(range(1))
             pick_rows(2)
-            send_rows(2)
+            row_copy(4).start()
 
         pick_rows(0)
         send_rows(0)
@@ -471,24 +509,25 @@
 
         @pl.when(s == 0)
         def _():
+            assign_slots(range(1, steps))
+            ids_start(range(1, steps))
+            edge_columns()
             rel_table[...] = dot_tn(relation[...], place[...]).astype(BF16)
 
         slot_count = negative_ids.shape[1]
         hits = onehot(iota((rows, slot_count), 0) == negative_ids[pl.ds(s, 1), :])
         counts[...] = dot_nt(jnp.ones((8, slot_count), BF16), hits)
         ar_cross(fetch)
+
+        @pl.when(s == 0)
+        def _():
+            row_copy(5).start()
+
         send_rows(3)
 
-        @pl.loop(0, groups // 4)
-        def _(k):
-            relations(k)
-
+        relations(0)
         ar_gather(fetch)
-
-        @pl.loop(groups // 4, groups // 2)
-        def _(k):
-            relations(k)
-
+        relations(1)
         ar_share(fetch)
         source_acc[...] = jnp.zeros_like(source_acc)
         count_row = counts[0:1, :]
@@ -496,13 +535,12 @@
         ar_done(fetch)
         block[...] = ar_read(fetch).astype(BF16)
 
-        @pl.loop(0, groups // 2)
-        def _(p):
-            base = pl.multiple_of(p * 2 * CAP, 2 * CAP)
-            here = pl.ds(base, 2 * CAP)
-            chosen = onehot(iota((2 * CAP, rows), 1) == slot_src[s, here, :])
+        @pl.loop(0, edges // (2 * CAP))
+        def _(k):
+            here = pl.ds(pl.multiple_of(k * 2 * CAP, 2 * CAP), 2 * CAP)
+            chosen = onehot(iota((2 * CAP, rows), 1) == edge_src[s, here, :])
             source = dot_nn(chosen, block[...])
-            q = times(source, rel_slots[here, :].astype(F32), main, first, sign).astype(BF16)
+            q = times(source, rel_edges[here, :].astype(F32), main, first, sign).astype(BF16)
             query[here, :] = q
             scores = jnp.where(present, dot_nt(q, table[...]), LOW)
             top = jnp.max(scores, 1, keepdims=True)
@@ -511,58 +549,52 @@
             neg_max[here, :] = top
             neg_sum[here, :] = jnp.sum(e, 1, keepdims=True)
 
-        @pl.loop(0, groups // 2)
-        def _(turn):
-            p = (turn + 2) % 3 * (1 - turn // 3) + turn // 3 * 3
-
-            for j in range(2):
-
-                @pl.when(2 * p + j > 0)
-                def _():
-                    row_copy(2 * p + j).wait_send()
-                    row_arrival(2 * p + j).wait_recv()
-
-            base = pl.multiple_of(p * 2 * CAP, 2 * CAP)
-            here = pl.ds(base, 2 * CAP)
+        collect(0)
+        collect(1)
+        collect(2)
+        collect(3)
+
+        @pl.loop(0, edges // (2 * CAP))
+        def _(k):
+            here = pl.ds(pl.multiple_of(k * 2 * CAP, 2 * CAP), 2 * CAP)
             q = query[here, :].astype(F32)
-            dest = jnp.concatenate(
-                [unpack(row_recv[s, 2 * p + j].astype(F32), CAP, main, tail) for j in range(2)], 0
-            )
-            positive = jnp.sum(q * dest, 1, keepdims=True)
+            positive = jnp.sum(q * dest[here, :], 1, keepdims=True)
             low = neg_max[here, :]
             top = jnp.maximum(low, positive)
             pos_exp = jnp.exp(positive - top)
             shrink = jnp.exp(low - top)
             total = pos_exp + neg_sum[here, :] * shrink
             coef_pos = pos_exp / total - 1.0
-            grad_dest = coef_pos * q
-            for j in range(2):
-                stack = pack(grad_dest[j * CAP : (j + 1) * CAP], main, tail)
-                grad_send[s, 2 * p + j] = stack.astype(BF16)
-
-            for j in range(2):
-
-                @pl.when((2 * p + j > 0) & (p < 3))
-                def _():
-                    grad_copy(2 * p + j).start()
-
-            coef_neg = (neg_exp[here, :] * (shrink / total)).astype(BF16)
-            weights[here, :] = coef_neg
-            grad_query = coef_pos * dest + dot_nn(coef_neg, table[...])
+            coef[here, :] = coef_pos
+            grad_dest[here, :] = (coef_pos * q).astype(BF16)
+            weights[here, :] = (neg_exp[here, :] * (shrink / total)).astype(BF16)
+
+        make_grads(2)
+        send_grads(2)
+
+        @pl.loop(0, edges // (2 * CAP))
+        def _(k):
+            base = pl.multiple_of(k * 2 * CAP, 2 * CAP)
+            here = pl.ds(base, 2 * CAP)
+            grad_query = coef[here, :] * dest[here, :] + dot_nn(weights[here, :], table[...])
             grad_source = times_conjugate(
-                grad_query, rel_slots[here, :].astype(F32), main, first, sign
+                grad_query, rel_edges[here, :].astype(F32), main, first, sign
             ).astype(BF16)
-            spread = onehot(iota((rows, 2 * CAP), 0) == src_rows[s, :, here])
+            spread = onehot(iota((rows, 2 * CAP), 0) == source_ids[pl.ds(s, 1), here])
             source_acc[...] += dot_nn(spread, grad_source)
 
         ar_fill(reduce, source_acc[...])
         ar_first(reduce)
+        make_grads(0)
+        send_grads(0)
         grad_recv[s, 0] = grad_send[s, 0]
         ar_scatter(reduce)
+        make_grads(1)
+        send_grads(1)
+        make_grads(3)
         grads[...] = dot_tn(weights[...], query[...])
         ar_cross(reduce)
-        grad_copy(6).start()
-        grad_copy(7).start()
+        send_grads(3)
         ar_gather(reduce)
 
         def scatter_grads(p):
@@ -579,6 +611,11 @@
         ar_share(reduce)
         scatter_grads(3)
         ar_done(reduce)
+
+        @pl.when(s == 0)
+        def _():
+            ids_wait(range(1, steps))
+
         total = grads[...] + jnp.where(m == root, ar_read(reduce), 0.0)
         fresh = state[...] + jnp.sum(total * total, 1, keepdims=True) * (1.0 / width)
         state[...] = fresh
@@ -626,19 +663,23 @@
             vmem((rows, wide), BF16),
             vmem((rows, 1), F32),
             vmem((relation.shape[0], wide), BF16),
-            vmem((steps, slots, 1), jnp.int32),
-            vmem((steps, slots, 1), jnp.int32),
-            vmem((steps, 1, slots), jnp.int32),
+            vmem((steps, edges, 1), jnp.int32),
+            vmem((steps, edges, 1), jnp.int32),
+            vmem((steps, 16, edges), BF16),
             vmem((steps, slots, edges), BF16),
-            vmem((groups, 8, CAP), jnp.int32),
-            vmem((groups, 8, CAP), jnp.int32),
+            vmem((steps, edges, slots), BF16),
+            vmem((steps, groups, 8, CAP), jnp.int32),
+            vmem((steps, groups, 8, CAP), jnp.int32),
             vmem((8, rows), F32),
-            vmem((slots, wide), BF16),
-            vmem((slots, wide), BF16),
-            vmem((slots, rows), F32),
-            vmem((slots, 1), F32),
-            vmem((slots, 1), F32),
-            vmem((slots, rows), BF16),
+            vmem((edges, wide), BF16),
+            vmem((edges, wide), BF16),
+            vmem((edges, rows), F32),
+            vmem((edges, 1), F32),
+            vmem((edges, 1), F32),
+            vmem((edges, rows), BF16),
+            vmem((edges, 1), F32),
+            vmem((edges, wide), F32),
+            vmem((edges, wide), BF16),
             vmem((steps, groups, stack, LANES), BF16),
             vmem((steps, groups, stack, LANES), BF16),
             vmem((steps, groups, stack, LANES), BF16),
@@ -653,8 +694,8 @@
             vmem((uses, piece, LANES), BF16),
             vmem((uses, piece, LANES), BF16),
             vmem((uses, 2, depth, piece, LANES), BF16),
-            dma((groups,)),
-            dma((groups,)),
+            dma((steps, groups)),
+            dma((steps, groups)),
             dma((steps, groups)),
             dma((steps, groups)),
             dma((steps, groups)),

time: 123 us -> 117 us (0.951); the launches traced: 123 us -> 115 us
  Pallas kernels: 120 us -> 111 us
    pallas_call x1, Pallas kernels: 120 us -> 111 us  [per_device(): pl.pallas_call(functools.partial(kernel, groups, members), out_shape=(jax...]
where the time goes in v4:
time: 117 us; the launch traced here: 115 us
  Pallas kernels  111 us (95%)
  local copies, waits for them, and re-layouts  3.02 us (3%)
    pallas_call x1, Pallas kernels, per_device(): pl.pallas_call(functools.partial(kernel, groups, members), out_shape=(jax...  111 us
    unnamed x2, local copies, waits for them, and re-layouts  3.02 us

profile of v4, /device:TPU:13, one launch (start us, length us, event | category | flops | bytes accessed | tf_op | source)
XLA Modules:
  0.0 115.1 jit_solution(4950868935821589769)
XLA Ops:
  0.6 111.5 %shard_map.104 = (bf16[800,256]{1,0:T(8,128)(2,1)}, f32[1,256]{1,0:T(1,128)}) custom-call(s32[2,8]{1,0:T(2,128)} %owners.1, bf16[800,256]{1,0:T(8,128)(2,1)} %bitcast.7, f32[1,256]{1,0:T(1,128)} %bitcast.10, bf16[800,1345]{1,0:T(8,128)(2,1)} %bitcast.6, s32[2,512]{1,0:T(2,128)} %source_ids.1, s32[2,512]{1,0:T(2,128)} %relation_ids.1, s32[2,1,512]{2,1,0:T(1,128)} %bitcast.9, ...), custom_call_target="tpu_custom_call" | custom-call | tf_op jit(solution)/shard_map/pallas_call | solution.py:653
  112.1 1.8 %copy.13 = bf16[256,800]{0,1:T(8,128)(2,1)} copy(bf16[256,800]{0,1:T(8,128)(2,1)} %bitcast.8) | data formatting | bytes 819200
  113.9 1.2 %copy.14 = f32[256]{0:T(256)} copy(f32[256]{0:T(256)} %bitcast.11) | data formatting | bytes 2048

commit v5 on v4

--- a/solution.py
+++ b/solution.py
@@ -100,6 +100,8 @@
     place,
     table,
     state,
+    rel_raw,
+    rel_sem,
     rel_table,
     edge_src,
     edge_rel,
@@ -195,6 +197,8 @@
         )
 
     barrier = pltpu.get_barrier_semaphore()
+    fetch_relation = pltpu.make_async_copy(relation, rel_raw, rel_sem)
+    fetch_relation.start()
 
     for k in range(1, groups):
         pl.semaphore_signal(barrier, inc=1, device_id=(peer(k), m), device_id_type=MESH)
@@ -512,7 +516,8 @@
             assign_slots(range(1, steps))
             ids_start(range(1, steps))
             edge_columns()
-            rel_table[...] = dot_tn(relation[...], place[...]).astype(BF16)
+            fetch_relation.wait()
+            rel_table[...] = dot_tn(rel_raw[...], place[...]).astype(BF16)
 
         slot_count = negative_ids.shape[1]
         hits = onehot(iota((rows, slot_count), 0) == negative_ids[pl.ds(s, 1), :])
@@ -623,6 +628,11 @@
 
     entity_out[...] = dot_nt(place[...], table[...]).astype(BF16)
     state_out[...] = jnp.sum(jnp.where(eye, state[...], 0.0), 0, keepdims=True)
+
+
+def hand_over(table, state, table_out, state_out):
+    table_out[...] = table[...]
+    state_out[...] = state[...]
 
 
 def per_device(
@@ -656,12 +666,20 @@
             jax.ShapeDtypeStruct((width, rows), BF16),
             jax.ShapeDtypeStruct((1, rows), F32),
         ),
-        in_specs=[pl.BlockSpec(memory_space=pltpu.SMEM)] + [whole] * 8,
+        in_specs=[
+            pl.BlockSpec(memory_space=pltpu.SMEM),
+            whole,
+            whole,
+            pl.BlockSpec(memory_space=pl.ANY),
+        ]
+        + [whole] * 5,
         out_specs=(whole, whole),
         scratch_shapes=[
             vmem((width, wide), BF16),
             vmem((rows, wide), BF16),
             vmem((rows, 1), F32),
+            vmem((width, relation.shape[0]), BF16),
+            dma(()),
             vmem((relation.shape[0], wide), BF16),
             vmem((steps, edges, 1), jnp.int32),
             vmem((steps, edges, 1), jnp.int32),
@@ -725,6 +743,15 @@
         dest_rows,
         negative_ids,
     )
+    table, state = pl.pallas_call(
+        hand_over,
+        out_shape=(
+            jax.ShapeDtypeStruct((width, rows), BF16),
+            jax.ShapeDtypeStruct((1, rows), F32),
+        ),
+        in_specs=[whole, whole],
+        out_specs=(whole, whole),
+    )(table, state)
     return (table.T, state.reshape(rows))
 
 

time: 117 us -> 115 us (0.983)
  local copies, waits for them, and re-layouts: 3.02 us -> 0 us
  Pallas kernels: 111 us -> 113 us
    unnamed x2 -> x0, local copies, waits for them, and re-layouts: 3.02 us -> none
    pallas_call x0 -> x1, Pallas kernels: none -> 1.79 us  [per_device(): pl.pallas_call(hand_over, out_shape=(jax.ShapeDtypeStruct((width, rows),...]
where the time goes in v5:
time: 115 us; the launch traced here: 114 us
  Pallas kernels  113 us (98%)
    pallas_call x1, Pallas kernels, per_device(): pl.pallas_call(functools.partial(kernel, groups, members), out_shape=(jax...  111 us

profile of v5, /device:TPU:13, one launch (start us, length us, event | category | flops | bytes accessed | tf_op | source)
XLA Modules:
  0.0 113.9 jit_solution(2399522931805257361)
XLA Ops:
  0.6 111.5 %shard_map.104 = (bf16[800,256]{1,0:T(8,128)(2,1)}, f32[1,256]{1,0:T(1,128)}) custom-call(s32[2,8]{1,0:T(2,128)} %owners.1, bf16[800,256]{1,0:T(8,128)(2,1)} %bitcast.7, f32[1,256]{1,0:T(1,128)} %bitcast.9, bf16[800,1345]{1,0:T(8,128)(2,1)} %bitcast.6, s32[2,512]{1,0:T(2,128)} %source_ids.1, s32[2,512]{1,0:T(2,128)} %relation_ids.1, s32[2,1,512]{2,1,0:T(1,128)} %bitcast.8, ...), custom_call_target="tpu_custom_call" | custom-call | tf_op jit(solution)/shard_map/pallas_call | solution.py:663
  112.1 1.8 %shard_map.105 = (bf16[800,256]{1,0:T(8,128)(2,1)}, f32[1,256]{1,0:T(1,128)}) custom-call(bf16[800,256]{1,0:T(8,128)(2,1)} %get-tuple-element.6.table, f32[1,256]{1,0:T(1,128)} %get-tuple-element.7.state), custom_call_target="tpu_custom_call" | custom-call | tf_op jit(solution)/shard_map/pallas_call | solution.py:746

commit v6 on v5

--- a/solution.py
+++ b/solution.py
@@ -174,6 +174,8 @@
     hops = [(0, j) for j in range(rings)]
     hops += sorted(((1, j) for j in range(rings)), key=lambda hop: -min(hop[1], rings - hop[1]))
 
+    blocks = ((0, 1), (2, 3), (4, 6), (5, 7))
+
     def peer(k):
         return ((gx + hops[k][0]) % 2) * rings + (gy + hops[k][1]) % rings
 
@@ -448,12 +450,12 @@
                 (peer(k), m),
             )
 
-        def asked(p):
-            ids = [ids_recv[s, 2 * p + j, 0:1, :] for j in range(2)]
+        def asked(ks):
+            ids = [ids_recv[s, k, 0:1, :] for k in ks]
             return onehot(iota((rows, 2 * CAP), 0) == jnp.concatenate(ids, 1))
 
         def pick_rows(p):
-            picked = dot_tn(asked(p), table[...])
+            picked = dot_tn(asked((2 * p, 2 * p + 1)), table[...])
             for j in range(2):
                 row_send[s, 2 * p + j] = pack(picked[j * CAP : (j + 1) * CAP], main, tail).astype(BF16)
 
@@ -467,15 +469,16 @@
             chosen = onehot(iota((2 * CAP, rel_rows), 1) == edge_rel[s, here, :])
             rel_edges[here, :] = dot_nn(chosen, rel_table[...]).astype(BF16)
 
-        def collect(p):
-            for k in (2 * p, 2 * p + 1):
+        def collect(ks):
+            for k in ks:
                 if k:
                     row_copy(k).wait_send()
                     row_arrival(k).wait_recv()
-            arrived = [unpack(row_recv[s, k].astype(F32), CAP, main, tail) for k in (2 * p, 2 * p + 1)]
+            arrived = [unpack(row_recv[s, k].astype(F32), CAP, main, tail) for k in ks]
             arrived = jnp.concatenate(arrived, 0).astype(BF16)
-            sorted_rows = dot_nn(given[s, :, 2 * p * CAP : (2 * p + 2) * CAP], arrived)
-            dest[...] = sorted_rows if p == 0 else dest[...] + sorted_rows
+            into = jnp.concatenate([given[s, :, k * CAP : (k + 1) * CAP] for k in ks], 1)
+            sorted_rows = dot_nn(into, arrived)
+            dest[...] = dest[...] + sorted_rows if ks[0] else sorted_rows
 
         def make_grads(p):
             block_rows = taken[s, 2 * p * CAP : (2 * p + 2) * CAP, :]
@@ -554,10 +557,8 @@
             neg_max[here, :] = top
             neg_sum[here, :] = jnp.sum(e, 1, keepdims=True)
 
-        collect(0)
-        collect(1)
-        collect(2)
-        collect(3)
+        for ks in blocks:
+            collect(ks)
 
         @pl.loop(0, edges // (2 * CAP))
         def _(k):
@@ -602,19 +603,19 @@
         send_grads(3)
         ar_gather(reduce)
 
-        def scatter_grads(p):
-            for k in (2 * p, 2 * p + 1):
+        def scatter_grads(ks):
+            for k in ks:
                 if k:
                     grad_copy(k).wait_send()
                     grad_arrival(k).wait_recv()
-            arrived = [unpack(grad_recv[s, k].astype(F32), CAP, main, tail) for k in (2 * p, 2 * p + 1)]
-            grads[...] += dot_nn(asked(p), jnp.concatenate(arrived, 0).astype(BF16))
-
-        scatter_grads(2)
-        scatter_grads(0)
-        scatter_grads(1)
+            arrived = [unpack(grad_recv[s, k].astype(F32), CAP, main, tail) for k in ks]
+            grads[...] += dot_nn(asked(ks), jnp.concatenate(arrived, 0).astype(BF16))
+
+        for ks in blocks[:2]:
+            scatter_grads(ks)
         ar_share(reduce)
-        scatter_grads(3)
+        for ks in blocks[2:]:
+            scatter_grads(ks)
         ar_done(reduce)
 
         @pl.when(s == 0)

time: 115 us -> 115 us (level)
  no operation moved by 1% of the time
where the time goes in v6:
time: 115 us; the launch traced here: 114 us
  Pallas kernels  113 us (98%)
    pallas_call x1, Pallas kernels, per_device(): pl.pallas_call(functools.partial(kernel, groups, members), out_shape=(jax...  111 us

profile of v6, /device:TPU:13, one launch (start us, length us, event | category | flops | bytes accessed | tf_op | source)
XLA Modules:
  0.0 113.9 jit_solution(13537641644879445823)
XLA Ops:
  0.6 111.5 %shard_map.104 = (bf16[800,256]{1,0:T(8,128)(2,1)}, f32[1,256]{1,0:T(1,128)}) custom-call(s32[2,8]{1,0:T(2,128)} %owners.1, bf16[800,256]{1,0:T(8,128)(2,1)} %bitcast.7, f32[1,256]{1,0:T(1,128)} %bitcast.9, bf16[800,1345]{1,0:T(8,128)(2,1)} %bitcast.6, s32[2,512]{1,0:T(2,128)} %source_ids.1, s32[2,512]{1,0:T(2,128)} %relation_ids.1, s32[2,1,512]{2,1,0:T(1,128)} %bitcast.8, ...), custom_call_target="tpu_custom_call" | custom-call | tf_op jit(solution)/shard_map/pallas_call | solution.py:664
  112.1 1.8 %shard_map.105 = (bf16[800,256]{1,0:T(8,128)(2,1)}, f32[1,256]{1,0:T(1,128)}) custom-call(bf16[800,256]{1,0:T(8,128)(2,1)} %get-tuple-element.6.table, f32[1,256]{1,0:T(1,128)} %get-tuple-element.7.state), custom_call_target="tpu_custom_call" | custom-call | tf_op jit(solution)/shard_map/pallas_call | solution.py:747
